TPU v7x, 256 devices: a whole 4x4x8 slice. The times are simulated.
256 devices in a mesh: seq: 2 (over core), expert: 128 (over y, x, z).
Axes of the slice: x: 4, y: 4, z: 8, core: 2. Of those that a mesh axis runs over, the one named last changes fastest.
Arguments:
- tokens: bfloat16 [32768, 4096], P(('seq', 'expert')), may hold values from -6 to 6
- routes: int32 [32768, 2], P(('seq', 'expert')), may hold values from 0 to 127, all different within a row; in each aligned block of 128 rows (0 to 127, 128 to 255, ...) at most 3 rows name the same one
- route_probs: float32 [32768, 2], P(('seq', 'expert')), may hold values from 0.25 to 1
- gate_weight: bfloat16 [128, 4096, 768], P('expert', None, 'seq'), may hold values from -0.09375 to 0.09375
- up_weight: bfloat16 [128, 4096, 768], P('expert', None, 'seq'), may hold values from -0.09375 to 0.09375
- down_weight: bfloat16 [128, 768, 4096], P('expert', 'seq'), may hold values from -0.21875 to 0.21875
- grad_out: bfloat16 [32768, 4096], P(('seq', 'expert')), may hold values from -3 to 3
Outputs:
- grad_tokens: bfloat16 [32768, 4096], P(('seq', 'expert'))
- grad_probs: bfloat16 [32768, 2], P(('seq', 'expert'))
Inputs may be any that keep to these rules, and one draw needn't show every extreme that they name: `routes`: each token names 2 different experts. Among the tokens of one device no expert is named by more than 3 tokens, and in every draw some device names some expert exactly 3 times.
All inputs are finite; a program needn't handle non-finite values.
Results may differ from a plain program's by a relative error of at most 0.01.
Values may be sent and summed in bfloat16 or wider, within the bound.
No kernel may reach another device: no remote copies, remote signals or barrier semaphores. Data moves between devices by JAX's collectives and lax.ppermute only.
A program may use at most 128 MiB of HBM per device.

v0:
```python
import jax
import jax.numpy as jnp
from jax import lax
from jax.sharding import PartitionSpec as P


def expert_terms(rows_in, rows_grad, gate_w, up_w, down_w):
    contract = (((1,), (1,)), ((), ()))
    gating = jnp.dot(rows_in, gate_w, preferred_element_type=jnp.float32)
    lifted = jnp.dot(rows_in, up_w, preferred_element_type=jnp.float32)
    sigmoid = jax.nn.sigmoid(gating)
    active = gating * sigmoid
    hidden = (active * lifted).astype(jnp.bfloat16)
    grad_hidden = lax.dot_general(rows_grad, down_w, contract, preferred_element_type=jnp.float32)
    grad_prob = jnp.sum(hidden.astype(jnp.float32) * grad_hidden, axis=1)
    slope_term = sigmoid * (1.0 + gating * (1.0 - sigmoid))
    grad_gate = (grad_hidden * lifted * slope_term).astype(jnp.bfloat16)
    grad_up = (grad_hidden * active).astype(jnp.bfloat16)
    grad_rows = lax.dot_general(grad_gate, gate_w, contract, preferred_element_type=jnp.float32)
    grad_rows = grad_rows + lax.dot_general(
        grad_up, up_w, contract, preferred_element_type=jnp.float32
    )
    return (grad_rows, grad_prob)


def on_device(tokens, routes, route_probs, gate_weight, up_weight, down_weight, grad_out):
    tok_count, model_width = tokens.shape
    top_count = routes.shape[1]
    expert_count = lax.axis_size("expert")
    capacity = 3 * tok_count * top_count // (2 * expert_count)
    chosen = routes.reshape(-1)
    onehot = (chosen[:, None] == jnp.arange(expert_count, dtype=jnp.int32)[None, :]).astype(
        jnp.int32
    )
    before = jnp.cumsum(onehot, axis=0) - onehot
    position = jnp.sum(before * onehot, axis=1)
    slot_ids = chosen * capacity + position
    source = jnp.arange(tok_count * top_count, dtype=jnp.int32) // top_count
    blank_rows = jnp.zeros((expert_count * capacity, model_width), jnp.bfloat16)
    send_in = (
        blank_rows.at[slot_ids].set(tokens[source]).reshape(expert_count, capacity, model_width)
    )
    send_grad = (
        blank_rows.at[slot_ids].set(grad_out[source]).reshape(expert_count, capacity, model_width)
    )
    recv_in, recv_grad = (
        lax.all_to_all(send_in, "expert", split_axis=0, concat_axis=0, tiled=True),
        lax.all_to_all(send_grad, "expert", split_axis=0, concat_axis=0, tiled=True),
    )
    both_in, both_grad = (
        lax.all_gather(recv_in, "seq", axis=0, tiled=True),
        lax.all_gather(recv_grad, "seq", axis=0, tiled=True),
    )
    part_rows, part_prob = expert_terms(
        both_in.reshape(-1, model_width),
        both_grad.reshape(-1, model_width),
        gate_weight[0],
        up_weight[0],
        down_weight[0],
    )
    rows_total = both_in.shape[0]
    grad_rows, grad_prob = (
        lax.psum_scatter(
            part_rows.reshape(rows_total, capacity, model_width).astype(jnp.bfloat16),
            "seq",
            scatter_dimension=0,
            tiled=True,
        ).astype(jnp.float32),
        lax.psum_scatter(
            part_prob.reshape(rows_total, capacity).astype(jnp.bfloat16),
            "seq",
            scatter_dimension=0,
            tiled=True,
        ).astype(jnp.float32),
    )
    out_rows = grad_rows.astype(jnp.bfloat16)
    out_prob = grad_prob.astype(jnp.bfloat16)
    back_rows, back_prob = (
        lax.all_to_all(out_rows, "expert", split_axis=0, concat_axis=0, tiled=True),
        lax.all_to_all(out_prob, "expert", split_axis=0, concat_axis=0, tiled=True),
    )
    picked = back_rows.reshape(-1, model_width)[slot_ids].reshape(tok_count, top_count, model_width)
    grad_tokens = jnp.sum(picked.astype(jnp.float32) * route_probs[:, :, None], axis=1).astype(
        jnp.bfloat16
    )
    grad_probs = back_prob.reshape(-1)[slot_ids].reshape(tok_count, top_count)
    return (grad_tokens, grad_probs)


def solution(mesh):
    placed = (
        P(("seq", "expert"), None),
        P(("seq", "expert"), None),
        P(("seq", "expert"), None),
        P("expert", None, "seq"),
        P("expert", None, "seq"),
        P("expert", "seq", None),
        P(("seq", "expert"), None),
    )
    return jax.shard_map(
        on_device,
        mesh=mesh,
        in_specs=placed,
        out_specs=(P(("seq", "expert"), None), P(("seq", "expert"), None)),
        check_vma=False,
    )
```

profile of v0, /device:TPU:32, one launch (start us, length us, event | category | flops | bytes accessed | tf_op | source)
XLA Modules:
  0.0 575.5 jit_solution(1240934103222674699)
XLA Ops:
  7.2 0.9 copy.18
  8.2 0.1 eq.29
  8.3 0.1 eq.25
  8.4 0.7 broadcast_multiply_fusion
  9.1 0.1 copy.20
  9.3 0.2 fusion.18
  9.6 0.1 copy.17
  9.7 0.1 mul.53
  9.8 0.2 fusion.20
  10.0 11.0 %scatter_custom_fusion.1 = bf16[384,4096]{1,0:T(8,128)(2,1)} fusion(s32[256]{0:T(256)S(1)} %bitcast.41, bf16[128,4096]{1,0:T(8,128)(2,1)} %param.7, s32[1024]{0:T(1024)S(1)} %pad_clamp_fusion.1, bf16[]{:T(256)} %constant.25.clone.1), kind=kCustom, calls=%fused_computation.17 | custom fusion | bytes 3146240 | tf_op jit(solution)/shard_map/scatter | solution.py:41
  21.0 7.1 %reshape.128 = bf16[128,3,4096]{2,1,0:T(4,128)(2,1)} reshape(bf16[384,4096]{1,0:T(8,128)(2,1)} %scatter_custom_fusion.1) | data formatting | bytes 6291456 | tf_op jit(solution)/shard_map/reshape | solution.py:41
  28.1 113.9 %all_to_all.24 = bf16[128,3,4096]{2,1,0:T(4,128)(2,1)S(1)} all-to-all(bf16[128,3,4096]{2,1,0:T(4,128)(2,1)} %reshape.128), channel_id=1, replica_groups=mesh['seq'=2,'expert'=128] {'expert'}, dimensions={0} | all-to-all | bytes 6291456 | tf_op jit(solution)/shard_map/all_to_all | solution.py:47
  142.0 3.9 copy.24
  146.0 0.0 all-gather.3.cloned.1.call-start
  146.0 10.9 %scatter_custom_fusion = bf16[384,4096]{1,0:T(8,128)(2,1)} fusion(s32[256]{0:T(256)S(1)} %bitcast.42, bf16[128,4096]{1,0:T(8,128)(2,1)} %param.13, s32[1024]{0:T(1024)S(1)} %pad_clamp_fusion.1, bf16[]{:T(256)} %constant.25.clone.1), kind=kCustom, calls=%fused_computation.19 | custom fusion | bytes 3146240 | tf_op jit(solution)/shard_map/scatter | solution.py:44
  156.9 7.2 %reshape.126 = bf16[128,3,4096]{2,1,0:T(4,128)(2,1)} reshape(bf16[384,4096]{1,0:T(8,128)(2,1)} %scatter_custom_fusion) | data formatting | bytes 6291456 | tf_op jit(solution)/shard_map/reshape | solution.py:44
  164.1 103.6 %all_to_all.25 = bf16[128,3,4096]{2,1,0:T(4,128)(2,1)S(1)} all-to-all(bf16[128,3,4096]{2,1,0:T(4,128)(2,1)} %reshape.126), channel_id=1, replica_groups=mesh['seq'=2,'expert'=128] {'expert'}, dimensions={0} | all-to-all | bytes 6291456 | tf_op jit(solution)/shard_map/all_to_all | solution.py:48
  267.7 3.9 copy.22
  271.7 0.0 reduce-scatter.2.cloned.1.call-start
  271.7 12.4 %copy.25 = bf16[256,3,4096]{2,1,0:T(4,128)(2,1)} copy(bf16[256,3,4096]{2,0,1:T(8,128)(2,1)} %all-gather.5.cloned.1.call-done) | data formatting | bytes 12582912 | tf_op jit(solution)/shard_map/all_gather | solution.py:51
  284.1 14.1 %reshape.129 = bf16[768,4096]{1,0:T(8,128)(2,1)} reshape(bf16[256,3,4096]{2,1,0:T(4,128)(2,1)} %copy.25) | data formatting | bytes 12582912 | tf_op jit(solution)/shard_map/reshape | solution.py:55
  298.3 6.6 %fusion.2 = f32[768,384]{0,1:T(8,128)} fusion(bf16[768,4096]{1,0:T(8,128)(2,1)} %reshape.129, bf16[1,4096,384]{2,1,0:T(8,128)(2,1)S(1)} %copy-done), kind=kOutput, calls=%fused_computation.10 | convolution fusion | flops 2415919104 | bytes 10616832 | tf_op jit(solution)/shard_map/dot_general | solution.py:9
  304.9 3.7 fusion.5
  308.6 11.4 %copy.23 = bf16[256,3,4096]{2,1,0:T(4,128)(2,1)} copy(bf16[256,3,4096]{2,0,1:T(8,128)(2,1)} %all-gather.3.cloned.1.call-done) | data formatting | bytes 12582912 | tf_op jit(solution)/shard_map/all_gather | solution.py:52
  320.0 13.9 %reshape.127 = bf16[768,4096]{1,0:T(8,128)(2,1)} reshape(bf16[256,3,4096]{2,1,0:T(4,128)(2,1)} %copy.23) | data formatting | bytes 12582912 | tf_op jit(solution)/shard_map/reshape | solution.py:56
  333.9 7.2 %multiply_reduce_fusion.1 = (bf16[768]{0:T(1024)(128)(2,1)S(1)}, f32[768,384]{0,1:T(8,128)S(1)}) fusion(f32[768,384]{0,1:T(8,128)} %fusion.5, f32[768,384]{0,1:T(8,128)} %fusion.2, bf16[768,4096]{1,0:T(8,128)(2,1)} %reshape.127, bf16[1,384,4096]{2,1,0:T(8,128)(2,1)} %param.12), kind=kOutput, calls=%fused_computation.23 | convolution fusion | flops 2418572544 | bytes 12977664 | tf_op jit(solution)/shard_map/dot_general | solution.py:14
  341.2 6.8 %fusion = f32[768,4096]{1,0:T(8,128)} fusion(bf16[1,4096,384]{2,1,0:T(8,128)(2,1)S(1)} %copy-done, f32[768,384]{0,1:T(8,128)S(1)} %copy-done.2, f32[768,384]{0,1:T(8,128)S(1)} %get-tuple-element.7, f32[768,384]{0,1:T(8,128)S(1)} %copy-done.5), kind=kOutput, calls=%fused_computation.8 | convolution fusion | flops 2418868224 | bytes 19267584 | tf_op jit(solution)/shard_map/dot_general | solution.py:19
  348.0 0.9 convert_element_type.56
  348.9 12.4 %add_convert_fusion = bf16[768,4096]{1,0:T(8,128)(2,1)} fusion(f32[768,4096]{1,0:T(8,128)} %fusion, bf16[1,4096,384]{2,1,0:T(8,128)(2,1)} %param.11, f32[768,384]{0,1:T(8,128)} %copy-done.3, f32[768,384]{0,1:T(8,128)} %fusion.2), kind=kOutput, calls=%fused_computation.6 | convolution fusion | flops 2423980032 | bytes 24379392 | tf_op jit(solution)/shard_map/dot_general | solution.py:20
  361.3 12.9 %convert_element_type.49 = bf16[256,3,4096]{2,1,0:T(4,128)(2,1)} reshape(bf16[768,4096]{1,0:T(8,128)(2,1)} %add_convert_fusion) | data formatting | bytes 12582912 | tf_op jit(solution)/shard_map/convert_element_type | solution.py:64
  374.3 0.6 copy-done.7
  374.9 0.6 dynamic-slice
  376.2 1.4 copy.27
  377.6 6.3 %all-to-all-start.3 = ((bf16[128,1,3]{2,1,0:T(2,128)(2,1)}), bf16[128,1,3]{2,1,0:T(2,128)(2,1)S(1)}, u32[]{:S(2)}, u32[]{:S(2)}) async-start(bf16[128,1,3]{2,1,0:T(2,128)(2,1)} %copy.27), calls=%async_computation.4 | async-start | bytes 131072 | tf_op jit(solution)/shard_map/all_to_all | solution.py:80
  384.0 33.0 %all-reduce.3.cloned.1.call-done = bf16[256,3,4096]{2,1,0:T(4,128)(2,1)} async-done(((bf16[256,3,4096]{2,1,0:T(4,128)(2,1)}), bf16[256,3,4096]{2,1,0:T(4,128)(2,1)}) %all-reduce.3.cloned.1.call-update) | async-done | bytes 6291472
  417.0 7.9 %constant_dynamic-slice_fusion = bf16[128,3,4096]{2,1,0:T(4,128)(2,1)} fusion(bf16[256,3,4096]{2,1,0:T(4,128)(2,1)} %all-reduce.3.cloned.1.call-done, u32[]{:T(128)S(6)} %multiply.1), kind=kLoop, calls=%fused_computation.48 | loop fusion | bytes 6291460
  424.8 14.5 %all-to-all-start.2 = ((bf16[128,3,4096]{2,1,0:T(4,128)(2,1)}), bf16[128,3,4096]{2,1,0:T(4,128)(2,1)}, u32[]{:S(2)}, u32[]{:S(2)}) async-start(bf16[128,3,4096]{2,1,0:T(4,128)(2,1)} %constant_dynamic-slice_fusion), calls=%async_computation.2 | async-start | bytes 8388608 | tf_op jit(solution)/shard_map/all_to_all | solution.py:79
  439.3 0.1 copy.26
  439.5 0.2 reduce
  439.7 0.2 reshape.131
  439.9 1.9 gather_fusion.1
  441.8 0.2 reshape.132
  442.0 0.6 copy.28
  442.6 95.6 %all-to-all-done.2 = bf16[128,3,4096]{2,1,0:T(4,128)(2,1)} async-done(((bf16[128,3,4096]{2,1,0:T(4,128)(2,1)}), bf16[128,3,4096]{2,1,0:T(4,128)(2,1)}, u32[]{:S(2)}, u32[]{:S(2)}) %all-to-all-start.2) | async-done | bytes 3145760 | tf_op jit(solution)/shard_map/all_to_all | solution.py:79
  538.2 7.4 %reshape.130 = bf16[384,4096]{1,0:T(8,128)(2,1)} reshape(bf16[128,3,4096]{2,1,0:T(4,128)(2,1)} %all-to-all-done.2) | data formatting | bytes 6291456 | tf_op jit(solution)/shard_map/reshape | solution.py:82
  545.6 7.6 %gather_fusion = bf16[256,4096]{1,0:T(8,128)(2,1)} fusion(bf16[384,4096]{1,0:T(8,128)(2,1)} %reshape.130, s32[1024]{0:T(1024)S(1)} %pad_clamp_fusion), kind=kCustom, calls=%fused_computation.2 | custom fusion | bytes 4195328 | tf_op jit(solution)/shard_map/gather | solution.py:82
  553.2 5.7 reshape.133
  558.9 9.6 %multiply_reduce_fusion = bf16[128,4096]{1,0:T(8,128)(2,1)} fusion(f32[128,2,4096]{2,1,0:T(2,128)} %reshape.133, f32[128,2]{1,0:T(8,128)S(1)} %copy.26), kind=kLoop, calls=%fused_computation.7 | loop fusion | flops 1572864 | bytes 5243904 | tf_op jit(solution)/shard_map/reduce_sum | solution.py:83
  (35 shorter events, 0.3 us)
Async XLA Ops:
  7.2 291.1 %copy-start = (bf16[1,4096,384]{2,1,0:T(8,128)(2,1)S(1)}, bf16[1,4096,384]{2,1,0:T(8,128)(2,1)}, u32[]{:S(2)}) copy-start(bf16[1,4096,384]{2,1,0:T(8,128)(2,1)} %param.10) | copy-start | bytes 9437188
  7.2 264.6 %all-gather.5.cloned.1.call-start = ((), (), s32[]{:S(2)}) async-start(), calls=%async_computation.6 | async-start | bytes 9437184 | tf_op jit(solution)/shard_map/all_gather | solution.py:51
  146.0 162.6 %all-gather.3.cloned.1.call-start = ((), (), s32[]{:S(2)}) async-start(), calls=%async_computation.5 | async-start | bytes 9437184 | tf_op jit(solution)/shard_map/all_gather | solution.py:52
  271.7 104.5 %reduce-scatter.2.cloned.1.call-start = ((), (), s32[]{:S(2)}) async-start(), calls=%async_computation.7 | async-start | bytes 98304 | tf_op jit(solution)/shard_map/reduce_scatter | solution.py:69
  298.3 6.6 %copy-start.1 = (bf16[768,4096]{1,0:T(8,128)(2,1)S(1)}, bf16[768,4096]{1,0:T(8,128)(2,1)}, u32[]{:S(2)}) copy-start(bf16[768,4096]{1,0:T(8,128)(2,1)} %reshape.129) | copy-start | bytes 18874372
  298.3 6.6 %copy-start.4 = (bf16[1,4096,384]{2,1,0:T(8,128)(2,1)S(1)}, bf16[1,4096,384]{2,1,0:T(8,128)(2,1)}, u32[]{:S(2)}) copy-start(bf16[1,4096,384]{2,1,0:T(8,128)(2,1)} %param.11) | copy-start | bytes 9437188
  333.9 7.3 %copy-start.2 = (f32[768,384]{0,1:T(8,128)S(1)}, f32[768,384]{0,1:T(8,128)}, u32[]{:S(2)}) copy-start(f32[768,384]{0,1:T(8,128)} %fusion.2) | copy-start | bytes 3538948
  333.9 7.3 %copy-start.5 = (f32[768,384]{0,1:T(8,128)S(1)}, f32[768,384]{0,1:T(8,128)}, u32[]{:S(2)}) copy-start(f32[768,384]{0,1:T(8,128)} %fusion.5) | copy-start | bytes 3538948
  341.1 6.8 %copy-start.3 = (f32[768,384]{0,1:T(8,128)}, f32[768,384]{0,1:T(8,128)S(1)}, u32[]{:S(2)}) copy-start(f32[768,384]{0,1:T(8,128)S(1)} %get-tuple-element.7) | copy-start | bytes 3538948
  348.9 68.1 %all-reduce.3.cloned.1.call-start = ((), (), s32[]{:S(2)}) async-start(), calls=%async_computation.8 | async-start | bytes 16777216
  374.2 0.7 copy-start.7
  377.6 47.2 %all-to-all-start.3 = ((bf16[128,1,3]{2,1,0:T(2,128)(2,1)}), bf16[128,1,3]{2,1,0:T(2,128)(2,1)S(1)}, u32[]{:S(2)}, u32[]{:S(2)}) async-start(bf16[128,1,3]{2,1,0:T(2,128)(2,1)} %copy.27), calls=%async_computation.4 | async-start | bytes 131072 | tf_op jit(solution)/shard_map/all_to_all | solution.py:80
  424.8 14.5 %copy-start.6 = (f32[128,2]{0,1:T(2,128)S(1)}, f32[128,2]{0,1:T(2,128)}, u32[]{:S(2)}) copy-start(f32[128,2]{0,1:T(2,128)} %param.9) | copy-start | bytes 3076
  424.8 113.4 %all-to-all-start.2 = ((bf16[128,3,4096]{2,1,0:T(4,128)(2,1)}), bf16[128,3,4096]{2,1,0:T(4,128)(2,1)}, u32[]{:S(2)}, u32[]{:S(2)}) async-start(bf16[128,3,4096]{2,1,0:T(4,128)(2,1)} %constant_dynamic-slice_fusion), calls=%async_computation.2 | async-start | bytes 8388608 | tf_op jit(solution)/shard_map/all_to_all | solution.py:79
Sparse Core Ops, SparseCore 0:
  146.1 14.9 all-gather.4
  271.8 14.9 all-gather.2
  349.0 5.6 reduce-scatter.1
  374.4 42.5 all-reduce.2
where the time goes:
time: 586 us; the launch traced here: 575 us
  blocking collectives  218 us (37%)
  local copies, waits for them, and re-layouts  145 us (25%)
  waiting for transfers between devices  129 us (22%)
  matrix products  36.7 us (6%)
  starting transfers between devices  21 us (4%)
  between operations  15.1 us (3%)
  other arithmetic  11 us (2%)
    all_to_all x1, blocking collectives, on_device(): lax.all_to_all(send_in, 'expert', split_axis=0, concat_axis=0, tiled=True)  114 us
    all_to_all x1, blocking collectives, on_device(): lax.all_to_all(send_grad, 'expert', split_axis=0, concat_axis=0, tiled=True)  104 us
    all_to_all x1, waiting for transfers between devices, on_device(): lax.all_to_all(out_rows, 'expert', split_axis=0, concat_axis=0, tiled=True)  95.6 us
    unnamed x5, waiting for transfers between devices  33.1 us
    all_to_all x1, starting transfers between devices, on_device(): lax.all_to_all(out_rows, 'expert', split_axis=0, concat_axis=0, tiled=True)  14.5 us
    reshape x1, local copies, waits for them, and re-layouts, on_device(): both_in.reshape(-1, model_width)  14.1 us
    reshape x1, local copies, waits for them, and re-layouts, on_device(): both_grad.reshape(-1, model_width)  13.9 us
    convert_element_type x1, local copies, waits for them, and re-layouts, on_device(): part_rows.reshape(rows_total, capacity, model_width).astype(jnp.bfloat16)  12.9 us
  transfers between devices with their start and end apart: 6, of which 2 were waited for; matrix products, arithmetic and copies ran while one was open for 17% of the time, Pallas kernels for 0%

commit v1 on v0

v1 whole, which is shorter than its diff:
```python
import functools

import jax
import jax.numpy as jnp
from jax import lax
from jax.experimental import pallas as pl
from jax.experimental.pallas import tpu as pltpu
from jax.sharding import PartitionSpec as P

LANES = 128
CHUNK = 8
VMEM_LIMIT = 56 * 1024 * 1024


def params():
    return pltpu.CompilerParams(vmem_limit_bytes=VMEM_LIMIT)


def to_blocks(x_ref, wide):
    rows, width = x_ref.shape
    parts = width // LANES
    for c in range(parts):
        wide[pl.ds(c, rows, stride=parts), :] = x_ref[:, c * LANES : (c + 1) * LANES].astype(
            jnp.float32
        )


def route_kernel(capacity, routes_ref, x_ref, slots_ref, out_ref, counts, wide):
    top, tok_count = routes_ref.shape
    parts = x_ref.shape[1] // LANES
    out_ref[...] = jnp.zeros_like(out_ref)

    def clear(e, _):
        counts[e] = 0
        return 0

    lax.fori_loop(0, counts.shape[0], clear, 0)
    to_blocks(x_ref, wide)

    def place(t, _):
        row = wide[pl.ds(pl.multiple_of(t * parts, parts), parts), :].astype(jnp.bfloat16)
        for k in range(top):
            e = routes_ref[k, t]
            position = counts[e]
            counts[e] = position + 1
            slot = e * capacity + position
            slots_ref[k, t] = slot
            out_ref[slot] = row
        return 0

    lax.fori_loop(0, tok_count, place, 0)


def route_and_place(routes, x, expert_count, capacity):
    tok_count, width = x.shape
    top = routes.shape[0]
    parts = width // LANES
    return pl.pallas_call(
        functools.partial(route_kernel, capacity),
        out_shape=(
            jax.ShapeDtypeStruct((top, tok_count), jnp.int32),
            jax.ShapeDtypeStruct((expert_count * capacity, parts, LANES), jnp.bfloat16),
        ),
        in_specs=[
            pl.BlockSpec(memory_space=pltpu.SMEM),
            pl.BlockSpec(memory_space=pltpu.VMEM),
        ],
        out_specs=(
            pl.BlockSpec(memory_space=pltpu.SMEM),
            pl.BlockSpec(memory_space=pltpu.VMEM),
        ),
        scratch_shapes=[
            pltpu.SMEM((expert_count,), jnp.int32),
            pltpu.VMEM((tok_count * parts, LANES), jnp.float32),
        ],
        compiler_params=params(),
        name="route_and_place",
    )(routes, x)


def place_kernel(slots_ref, x_ref, out_ref, wide):
    top, tok_count = slots_ref.shape
    parts = x_ref.shape[1] // LANES
    out_ref[...] = jnp.zeros_like(out_ref)
    to_blocks(x_ref, wide)

    def place(t, _):
        row = wide[pl.ds(pl.multiple_of(t * parts, parts), parts), :].astype(jnp.bfloat16)
        for k in range(top):
            out_ref[slots_ref[k, t]] = row
        return 0

    lax.fori_loop(0, tok_count, place, 0)


def place_rows(slots, x, slot_count):
    tok_count, width = x.shape
    parts = width // LANES
    return pl.pallas_call(
        place_kernel,
        out_shape=jax.ShapeDtypeStruct((slot_count, parts, LANES), jnp.bfloat16),
        in_specs=[
            pl.BlockSpec(memory_space=pltpu.SMEM),
            pl.BlockSpec(memory_space=pltpu.VMEM),
        ],
        out_specs=pl.BlockSpec(memory_space=pltpu.VMEM),
        scratch_shapes=[pltpu.VMEM((tok_count * parts, LANES), jnp.float32)],
        compiler_params=params(),
        name="place_rows",
    )(slots, x)


def load_rows(x_ref, wide, rows_scr):
    rows = x_ref.shape[0]
    wide[...] = x_ref[...].astype(jnp.float32).reshape(rows * CHUNK, LANES)
    for c in range(CHUNK):
        rows_scr[:, c * LANES : (c + 1) * LANES] = wide[pl.ds(c, rows, stride=CHUNK), :].astype(
            jnp.bfloat16
        )


def forward_kernel(x_ref, g0, g1, u0, u1, hidden_ref, slope_ref, active_ref, wide, rows_scr, acc_g, acc_u):
    step = pl.program_id(0)

    @pl.when(step == 0)
    def _():
        acc_g[...] = jnp.zeros_like(acc_g)
        acc_u[...] = jnp.zeros_like(acc_u)

    load_rows(x_ref, wide, rows_scr)
    rows = rows_scr[...]
    gate = jnp.concatenate([g0[...], g1[...]], axis=1)
    acc_g[...] += jnp.dot(rows, gate, preferred_element_type=jnp.float32)
    up = jnp.concatenate([u0[...], u1[...]], axis=1)
    acc_u[...] += jnp.dot(rows, up, preferred_element_type=jnp.float32)

    @pl.when(step == pl.num_programs(0) - 1)
    def _():
        gating = acc_g[...]
        lifted = acc_u[...]
        sigmoid = jax.nn.sigmoid(gating)
        active = gating * sigmoid
        hidden_ref[...] = (active * lifted).astype(jnp.bfloat16)
        slope_ref[...] = lifted * (sigmoid * (1.0 + gating * (1.0 - sigmoid)))
        active_ref[...] = active


def forward_terms(x, g0, g1, u0, u1):
    rows, parts, _ = x.shape
    half = g0.shape[1]
    hid = 2 * half
    depth = CHUNK * LANES
    weight = pl.BlockSpec((depth, half), lambda i: (i, 0))
    whole = pl.BlockSpec((rows, hid), lambda i: (0, 0))
    return pl.pallas_call(
        forward_kernel,
        grid=(parts // CHUNK,),
        out_shape=(
            jax.ShapeDtypeStruct((rows, hid), jnp.bfloat16),
            jax.ShapeDtypeStruct((rows, hid), jnp.float32),
            jax.ShapeDtypeStruct((rows, hid), jnp.float32),
        ),
        in_specs=[pl.BlockSpec((rows, CHUNK, LANES), lambda i: (0, i, 0))] + [weight] * 4,
        out_specs=(whole, whole, whole),
        scratch_shapes=[
            pltpu.VMEM((rows * CHUNK, LANES), jnp.float32),
            pltpu.VMEM((rows, depth), jnp.bfloat16),
            pltpu.VMEM((rows, hid), jnp.float32),
            pltpu.VMEM((rows, hid), jnp.float32),
        ],
        compiler_params=params(),
        name="forward_terms",
    )(x, g0, g1, u0, u1)


def backward_kernel(
    half_steps, x_ref, d0, d1, g0, g1, u0, u1, hidden_ref, slope_ref, active_ref,
    out_ref, prob_ref, wide, rows_scr, acc, grad_gate, grad_up,
):
    step = pl.program_id(0)
    contract = (((1,), (1,)), ((), ()))

    @pl.when(step == 0)
    def _():
        acc[...] = jnp.zeros_like(acc)

    @pl.when(step < half_steps)
    def _():
        load_rows(x_ref, wide, rows_scr)
        down = jnp.concatenate([d0[...], d1[...]], axis=0)
        acc[...] += lax.dot_general(rows_scr[...], down, contract, preferred_element_type=jnp.float32)

    @pl.when(step == half_steps - 1)
    def _():
        grad_hidden = acc[...]
        prob = jnp.sum(hidden_ref[...].astype(jnp.float32) * grad_hidden, axis=1, keepdims=True)
        prob_ref[...] = jnp.broadcast_to(prob, prob_ref.shape).astype(jnp.bfloat16)
        grad_gate[...] = (grad_hidden * slope_ref[...]).astype(jnp.bfloat16)
        grad_up[...] = (grad_hidden * active_ref[...]).astype(jnp.bfloat16)

    @pl.when(step >= half_steps)
    def _():
        rows = x_ref.shape[0]
        gate = jnp.concatenate([g0[...], g1[...]], axis=1)
        total = lax.dot_general(grad_gate[...], gate, contract, preferred_element_type=jnp.float32)
        up = jnp.concatenate([u0[...], u1[...]], axis=1)
        total += lax.dot_general(grad_up[...], up, contract, preferred_element_type=jnp.float32)
        for c in range(CHUNK):
            wide[pl.ds(c, rows, stride=CHUNK), :] = total[:, c * LANES : (c + 1) * LANES]
        out_ref[...] = wide[...].reshape(rows, CHUNK, LANES).astype(jnp.bfloat16)


def backward_terms(x, d0, d1, g0, g1, u0, u1, hidden, slope, active):
    rows, parts, _ = x.shape
    half = g0.shape[1]
    hid = 2 * half
    depth = CHUNK * LANES
    steps = parts // CHUNK
    early = lambda i: jnp.minimum(i, steps - 1)
    late = lambda i: jnp.maximum(i - steps, 0)
    down = pl.BlockSpec((half, depth), lambda i: (0, early(i)))
    weight = pl.BlockSpec((depth, half), lambda i: (late(i), 0))
    whole = pl.BlockSpec((rows, hid), lambda i: (0, 0), pipeline_mode=pl.Buffered(1))
    return pl.pallas_call(
        functools.partial(backward_kernel, steps),
        grid=(2 * steps,),
        out_shape=(
            jax.ShapeDtypeStruct((rows, parts, LANES), jnp.bfloat16),
            jax.ShapeDtypeStruct((rows, LANES), jnp.bfloat16),
        ),
        in_specs=[pl.BlockSpec((rows, CHUNK, LANES), lambda i: (0, early(i), 0))]
        + [down] * 2
        + [weight] * 4
        + [whole] * 3,
        out_specs=(
            pl.BlockSpec((rows, CHUNK, LANES), lambda i: (0, late(i), 0)),
            pl.BlockSpec((rows, LANES), lambda i: (0, 0)),
        ),
        scratch_shapes=[
            pltpu.VMEM((rows * CHUNK, LANES), jnp.float32),
            pltpu.VMEM((rows, depth), jnp.bfloat16),
            pltpu.VMEM((rows, hid), jnp.float32),
            pltpu.VMEM((rows, hid), jnp.bfloat16),
            pltpu.VMEM((rows, hid), jnp.bfloat16),
        ],
        compiler_params=params(),
        name="backward_terms",
    )(x, d0, d1, g0, g1, u0, u1, hidden, slope, active)


def combine_kernel(slots_ref, probs_ref, back_ref, out_ref, wide):
    top, tok_count = slots_ref.shape
    parts = back_ref.shape[1]

    def gather(t, _):
        total = probs_ref[0, t] * back_ref[slots_ref[0, t]].astype(jnp.float32)
        for k in range(1, top):
            total += probs_ref[k, t] * back_ref[slots_ref[k, t]].astype(jnp.float32)
        wide[pl.ds(pl.multiple_of(t * parts, parts), parts), :] = total
        return 0

    lax.fori_loop(0, tok_count, gather, 0)
    for c in range(parts):
        out_ref[:, c * LANES : (c + 1) * LANES] = wide[pl.ds(c, tok_count, stride=parts), :].astype(
            jnp.bfloat16
        )


def combine_rows(slots, probs, back):
    top, tok_count = slots.shape
    parts = back.shape[1]
    return pl.pallas_call(
        combine_kernel,
        out_shape=jax.ShapeDtypeStruct((tok_count, parts * LANES), jnp.bfloat16),
        in_specs=[
            pl.BlockSpec(memory_space=pltpu.SMEM),
            pl.BlockSpec(memory_space=pltpu.SMEM),
            pl.BlockSpec(memory_space=pltpu.VMEM),
        ],
        out_specs=pl.BlockSpec(memory_space=pltpu.VMEM),
        scratch_shapes=[pltpu.VMEM((tok_count * parts, LANES), jnp.float32)],
        compiler_params=params(),
        name="combine_rows",
    )(slots, probs, back)


def exchange(blocks, expert_count):
    rows, parts, lanes = blocks.shape
    sent = blocks.reshape(expert_count, rows // expert_count * parts, lanes)
    got = lax.all_to_all(sent, "expert", split_axis=0, concat_axis=0, tiled=True)
    return got.reshape(rows, parts, lanes)


def on_device(tokens, routes, route_probs, gate_weight, up_weight, down_weight, grad_out):
    tok_count, model_width = tokens.shape
    top_count = routes.shape[1]
    expert_count = lax.axis_size("expert")
    capacity = 3 * tok_count * top_count // (2 * expert_count)
    swap = lambda w: lax.ppermute(w, "seq", [(0, 1), (1, 0)])
    gate, up, down = gate_weight[0], up_weight[0], down_weight[0]
    gate_far, up_far, down_far = swap(gate), swap(up), swap(down)

    slots, send_in = route_and_place(routes.T, tokens, expert_count, capacity)
    recv_in = exchange(send_in, expert_count)
    send_grad = place_rows(slots, grad_out, expert_count * capacity)
    recv_grad = exchange(send_grad, expert_count)
    hidden, slope, active = forward_terms(recv_in, gate, gate_far, up, up_far)
    out_rows, out_prob = backward_terms(
        recv_grad, down, down_far, gate, gate_far, up, up_far, hidden, slope, active
    )
    back_rows = exchange(out_rows, expert_count)
    grad_tokens = combine_rows(slots, route_probs.T, back_rows)

    all_prob = lax.all_gather(out_prob[:, 0], "expert", axis=0, tiled=False)
    mine = lax.dynamic_slice(
        all_prob, (0, lax.axis_index("expert") * capacity), (expert_count, capacity)
    )
    grad_probs = mine.reshape(-1)[slots.T]
    return (grad_tokens, grad_probs)


def solution(mesh):
    placed = (
        P(("seq", "expert"), None),
        P(("seq", "expert"), None),
        P(("seq", "expert"), None),
        P("expert", None, "seq"),
        P("expert", None, "seq"),
        P("expert", "seq", None),
        P(("seq", "expert"), None),
    )
    return jax.shard_map(
        on_device,
        mesh=mesh,
        in_specs=placed,
        out_specs=(P(("seq", "expert"), None), P(("seq", "expert"), None)),
        check_vma=False,
    )
```

time: 586 us -> 729 us (1.24); the launches traced: 575 us -> 728 us
  blocking collectives: 218 us -> 499 us
  local copies, waits for them, and re-layouts: 145 us -> 8.77 us
  Pallas kernels: 0 us -> 49.2 us
  matrix products: 36.7 us -> 0 us
  between operations: 15.1 us -> 0.77 us
  starting transfers between devices: 21 us -> 29.2 us
    all_gather x0 -> x1, blocking collectives: none -> 499 us  [on_device(): all_prob = lax.all_gather(out_prob[:, 0], 'expert', axis=0, tiled=False)]
    all_to_all x2 -> x0, blocking collectives: 218 us -> none  [the longest x1 114 us: on_device(): lax.all_to_all(send_in, 'expert', split_axis=0, concat_axis=0, tiled=True)]
    reshape x7 -> x1, local copies, waits for them, and re-layouts: 50.1 us -> 0.21 us  [on_device(): grad_probs = mine.reshape(-1)[slots.T]]
    pallas_call x0 -> x5, Pallas kernels: none -> 49.2 us  [the longest x1 17.4 us: backward_terms(): pl.pallas_call(functools.partial(backward_kernel, steps), grid=(2 * steps...]
    dot_general x5 -> x0, matrix products: 36.7 us -> none  [the longest x1 12.4 us: expert_terms(): lax.dot_general(grad_up, up_w, contract, preferred_element_type=jnp.float32)]
    unnamed x5 -> x0, waiting for transfers between devices: 33.1 us -> none
    all_to_all x2 -> x3, waiting for transfers between devices: 95.6 us -> 122 us  [exchange(): lax.all_to_all(sent, 'expert', split_axis=0, concat_axis=0, tiled=True)]
    all_gather x2 -> x1, local copies, waits for them, and re-layouts: 23.8 us -> 0.05 us  [on_device(): all_prob = lax.all_gather(out_prob[:, 0], 'expert', axis=0, tiled=False)]
  transfers between devices with their start and end apart: 6 -> 6, of which waited for: 2 -> 4; matrix products, arithmetic and copies ran while one was open for 17% -> 2% of each run, Pallas kernels for 0% -> 2%
where the time goes in v1:
time: 729 us; the launch traced here: 728 us
  blocking collectives  499 us (68%)
  waiting for transfers between devices  132 us (18%)
  Pallas kernels  49.2 us (7%)
  starting transfers between devices  29.2 us (4%)
  other arithmetic  9.62 us (1%)
  local copies, waits for them, and re-layouts  8.77 us (1%)
    all_gather x1, blocking collectives, on_device(): all_prob = lax.all_gather(out_prob[:, 0], 'expert', axis=0, tiled=False)  499 us
    all_to_all x3, waiting for transfers between devices, exchange(): lax.all_to_all(sent, 'expert', split_axis=0, concat_axis=0, tiled=True)  122 us
    all_to_all x3, starting transfers between devices, exchange(): lax.all_to_all(sent, 'expert', split_axis=0, concat_axis=0, tiled=True)  28.5 us
    pallas_call x1, Pallas kernels, backward_terms(): pl.pallas_call(functools.partial(backward_kernel, steps), grid=(2 * steps...  17.4 us
  transfers between devices with their start and end apart: 6, of which 4 were waited for; matrix products, arithmetic and copies ran while one was open for 2% of the time, Pallas kernels for 2%

profile of v1, /device:TPU:32, one launch (start us, length us, event | category | flops | bytes accessed | tf_op | source)
XLA Modules:
  0.0 728.3 jit_solution(14799121450142086732)
XLA Ops:
  0.6 7.9 %route_and_place.1 = (s32[2,128]{1,0:T(2,128)}, bf16[384,32,128]{2,1,0:T(8,128)(2,1)}) custom-call(s32[2,128]{1,0:T(2,128)} %bitcast.29, bf16[128,4096]{1,0:T(8,128)(2,1)} %x_ref.2), custom_call_target="tpu_custom_call" | custom-call | tf_op jit(solution)/shard_map/route_and_place/pallas_call | solution.py:58
  8.6 15.0 %all-to-all-start.1 = ((bf16[128,96,128]{2,1,0:T(8,128)(2,1)}), bf16[128,96,128]{2,1,0:T(8,128)(2,1)S(1)}, u32[]{:S(2)}, u32[]{:S(2)}) async-start(bf16[128,96,128]{2,1,0:T(8,128)(2,1)} %bitcast.27), calls=%async_computation.1 | async-start | bytes 6291456 | tf_op jit(solution)/shard_map/all_to_all | solution.py:290
  23.6 6.4 place_rows.1
  30.0 69.9 %all-to-all-done.1 = bf16[128,96,128]{2,1,0:T(8,128)(2,1)S(1)} async-done(((bf16[128,96,128]{2,1,0:T(8,128)(2,1)}), bf16[128,96,128]{2,1,0:T(8,128)(2,1)S(1)}, u32[]{:S(2)}, u32[]{:S(2)}) %all-to-all-start.1) | async-done | bytes 3145760 | tf_op jit(solution)/shard_map/all_to_all | solution.py:290
  99.9 0.0 copy-start.3
  99.9 1.6 copy-done.3
  101.6 6.7 all-to-all-start
  108.2 0.1 collective-permute-start.1
  108.3 0.5 collective-permute-start.2
  108.8 0.1 collective-permute-start
  108.9 8.7 %collective-permute-done.1.g1 = bf16[4096,384]{1,0:T(8,128)(2,1)S(1)} collective-permute-done((bf16[4096,384]{1,0:T(8,128)(2,1)}, bf16[4096,384]{1,0:T(8,128)(2,1)S(1)}, u32[]{:S(2)}, u32[]{:S(2)}) %collective-permute-start.1) | collective-permute-done | bytes 3145760 | tf_op jit(solution)/shard_map/ppermute | solution.py:299
  117.7 0.0 copy-start.2
  117.7 1.2 collective-permute-done.2.u1
  118.8 0.5 copy-done.2
  119.4 11.3 %forward_terms.1 = (bf16[384,768]{1,0:T(8,128)(2,1)}, f32[384,768]{1,0:T(8,128)}, f32[384,768]{1,0:T(8,128)}) custom-call(bf16[384,32,128]{2,1,0:T(8,128)(2,1)} %bitcast.23, bf16[4096,384]{1,0:T(8,128)(2,1)} %bitcast.18, bf16[4096,384]{1,0:T(8,128)(2,1)} %copy-done.2, bf16[4096,384]{1,0:T(8,128)(2,1)} %bitcast.21, bf16[4096,384]{1,0:T(8,128)(2,1)} %collective-permute-done.2.u1), custom_call_target="tpu_custom_call" | custom-call | tf_op jit(solution)/shard_map/forward_terms/pallas_call | solution.py:155
  130.7 0.0 collective-permute-done.d1
  130.7 52.1 %all-to-all-done = bf16[128,96,128]{2,1,0:T(8,128)(2,1)S(1)} async-done(((bf16[128,96,128]{2,1,0:T(8,128)(2,1)}), bf16[128,96,128]{2,1,0:T(8,128)(2,1)S(1)}, u32[]{:S(2)}, u32[]{:S(2)}) %all-to-all-start) | async-done | bytes 3145760 | tf_op jit(solution)/shard_map/all_to_all | solution.py:290
  182.7 0.0 copy-start
  182.8 1.6 copy-done
  184.4 17.4 %backward_terms.1 = (bf16[384,32,128]{2,1,0:T(8,128)(2,1)}, bf16[384,128]{1,0:T(8,128)(2,1)}) custom-call(bf16[384,32,128]{2,1,0:T(8,128)(2,1)} %bitcast.14, bf16[384,4096]{1,0:T(8,128)(2,1)} %bitcast.25, bf16[384,4096]{1,0:T(8,128)(2,1)} %collective-permute-done.d1, bf16[4096,384]{1,0:T(8,128)(2,1)} %bitcast.19, bf16[4096,384]{1,0:T(8,128)(2,1)} %copy-done.2, ...), custom_call_target="tpu_custom_call" | custom-call | tf_op jit(solution)/shard_map/backward_terms/pallas_call | solution.py:224
  201.8 0.0 copy-start.5
  201.8 0.0 copy-start.4
  201.8 6.8 all-to-all-start.2
  208.6 0.0 copy-done.5
  208.6 0.1 copy.9
  208.8 0.1 reshape.34
  208.9 0.0 copy-done.4
  208.9 498.9 %all-gather = bf16[49152,1]{1,0:T(8,128)(2,1)} all-gather(bf16[384,1]{1,0:T(8,128)(2,1)S(1)} %bitcast.28), channel_id=2, replica_groups=mesh['seq'=2,'expert'=128] {'expert'}, dimensions={0}, use_global_device_ids=true | all-gather | bytes 99072 | tf_op jit(solution)/shard_map/all_gather | solution.py:314
  707.8 9.6 %reduce = bf16[49152]{0:T(1024)(128)(2,1)S(1)} reduce(bf16[49152,1]{1,0:T(8,128)(2,1)} %all-gather, bf16[]{:T(256)} %constant.19), dimensions={1}, to_apply=%all-gather.reduce_sub_computation | reduce | bytes 196610 | tf_op jit(solution)/shard_map/all_gather | solution.py:314
  717.4 0.1 reshape.40
  717.5 0.1 constant_dynamic-slice_fusion
  717.6 0.2 reshape.31
  717.8 1.9 gather_fusion
  719.7 0.2 reshape.33
  719.9 0.6 copy.10
  720.5 0.0 all-to-all-done.2
  720.5 0.0 copy-start.1
  720.5 1.6 copy-done.1
  722.1 6.2 combine_rows.1
  (2 shorter events, 0.0 us)
Async XLA Ops:
  8.6 91.3 %all-to-all-start.1 = ((bf16[128,96,128]{2,1,0:T(8,128)(2,1)}), bf16[128,96,128]{2,1,0:T(8,128)(2,1)S(1)}, u32[]{:S(2)}, u32[]{:S(2)}) async-start(bf16[128,96,128]{2,1,0:T(8,128)(2,1)} %bitcast.27), calls=%async_computation.1 | async-start | bytes 6291456 | tf_op jit(solution)/shard_map/all_to_all | solution.py:290
  99.9 1.6 copy-start.3
  101.6 81.2 %all-to-all-start = ((bf16[128,96,128]{2,1,0:T(8,128)(2,1)}), bf16[128,96,128]{2,1,0:T(8,128)(2,1)S(1)}, u32[]{:S(2)}, u32[]{:S(2)}) async-start(bf16[128,96,128]{2,1,0:T(8,128)(2,1)} %bitcast.15), calls=%async_computation | async-start | bytes 6291456 | tf_op jit(solution)/shard_map/all_to_all | solution.py:290
  108.2 9.4 %collective-permute-start.1 = (bf16[4096,384]{1,0:T(8,128)(2,1)}, bf16[4096,384]{1,0:T(8,128)(2,1)S(1)}, u32[]{:S(2)}, u32[]{:S(2)}) collective-permute-start(bf16[4096,384]{1,0:T(8,128)(2,1)} %bitcast.17), channel_id=1, source_target_pairs={{0,128},{128,0},{1,129},{129,1},{2,130},{130,2},{3,131},{131,3},{4... | collective-permute-start | bytes 9437192 | tf_op jit(solution)/shard_map/ppermute | solution.py:299
  108.3 10.5 %collective-permute-start.2 = (bf16[4096,384]{1,0:T(8,128)(2,1)}, bf16[4096,384]{1,0:T(8,128)(2,1)}, u32[]{:S(2)}, u32[]{:S(2)}) collective-permute-start(bf16[4096,384]{1,0:T(8,128)(2,1)} %bitcast.20), channel_id=1, source_target_pairs={{0,128},{128,0},{1,129},{129,1},{2,130},{130,2},{3,131},{131,3},{4... | collective-permute-start | bytes 9437192 | tf_op jit(solution)/shard_map/ppermute | solution.py:299
  108.8 21.8 %collective-permute-start = (bf16[384,4096]{1,0:T(8,128)(2,1)}, bf16[384,4096]{1,0:T(8,128)(2,1)}, u32[]{:S(2)}, u32[]{:S(2)}) collective-permute-start(bf16[384,4096]{1,0:T(8,128)(2,1)} %bitcast.24), channel_id=1, source_target_pairs={{0,128},{128,0},{1,129},{129,1},{2,130},{130,2},{3,131},{131,3},{4... | collective-permute-start | bytes 9437192 | tf_op jit(solution)/shard_map/ppermute | solution.py:299
  117.7 1.7 copy-start.2
  182.7 1.6 copy-start
  201.8 6.9 copy-start.5
  201.8 7.1 copy-start.4
  201.8 518.7 %all-to-all-start.2 = ((bf16[128,96,128]{2,1,0:T(8,128)(2,1)}), bf16[128,96,128]{2,1,0:T(8,128)(2,1)S(1)}, u32[]{:S(2)}, u32[]{:S(2)}) async-start(bf16[128,96,128]{2,1,0:T(8,128)(2,1)} %bitcast.26), calls=%async_computation.2 | async-start | bytes 6291456 | tf_op jit(solution)/shard_map/all_to_all | solution.py:290
  720.5 1.6 copy-start.1

commit v2 on v1

v2 whole, which is shorter than its diff:
```python
import functools

import jax
import jax.numpy as jnp
from jax import lax
from jax.experimental import pallas as pl
from jax.experimental.pallas import tpu as pltpu
from jax.sharding import PartitionSpec as P

LANES = 128
CHUNK = 8
VMEM_LIMIT = 58 * 1024 * 1024
VMEM = pl.BlockSpec(memory_space=pltpu.VMEM)
SMEM = pl.BlockSpec(memory_space=pltpu.SMEM)


def params():
    return pltpu.CompilerParams(vmem_limit_bytes=VMEM_LIMIT)


def on_chip(x):
    return pltpu.with_memory_space_constraint(x, pltpu.VMEM)


def to_blocks(x_ref, wide, blocks):
    rows, width = x_ref.shape
    parts = width // LANES
    for c in range(parts):
        wide[pl.ds(c, rows, stride=parts), :] = x_ref[:, c * LANES : (c + 1) * LANES].astype(
            jnp.float32
        )
    blocks[...] = wide[...].reshape(rows, parts, LANES).astype(jnp.bfloat16)


def place_all(routes_ref, position_ref, blocks, out_ref, capacity):
    top, tok_count = routes_ref.shape
    group = 8

    def place(g, _):
        first = g * group
        rows = [blocks[first + i] for i in range(group)]
        slots = [
            [routes_ref[k, first + i] * capacity + position_ref[k, first + i] for k in range(top)]
            for i in range(group)
        ]
        for row, targets in zip(rows, slots):
            for slot in targets:
                out_ref[slot] = row
        return 0

    lax.fori_loop(0, tok_count // group, place, 0)


def route_kernel(capacity, routes_ref, x_ref, position_ref, out_ref, counts, wide, blocks):
    top, tok_count = routes_ref.shape

    def clear(e, _):
        counts[e] = 0
        return 0

    lax.fori_loop(0, counts.shape[0], clear, 0, unroll=16)
    to_blocks(x_ref, wide, blocks)

    def rank(t, _):
        for k in range(top):
            e = routes_ref[k, t]
            position = counts[e]
            counts[e] = position + 1
            position_ref[k, t] = position
        return 0

    lax.fori_loop(0, tok_count, rank, 0, unroll=8)
    place_all(routes_ref, position_ref, blocks, out_ref, capacity)


def route_and_place(routes, x, expert_count, capacity):
    tok_count, width = x.shape
    parts = width // LANES
    return pl.pallas_call(
        functools.partial(route_kernel, capacity),
        out_shape=(
            jax.ShapeDtypeStruct(routes.shape, jnp.int32),
            jax.ShapeDtypeStruct((expert_count * capacity, parts, LANES), jnp.bfloat16),
        ),
        in_specs=[SMEM, VMEM],
        out_specs=(SMEM, VMEM),
        scratch_shapes=[
            pltpu.SMEM((expert_count,), jnp.int32),
            pltpu.VMEM((tok_count * parts, LANES), jnp.float32),
            pltpu.VMEM((tok_count, parts, LANES), jnp.bfloat16),
        ],
        compiler_params=params(),
        name="route_and_place",
    )(routes, x)


def place_kernel(capacity, routes_ref, position_ref, x_ref, out_ref, wide, blocks):
    to_blocks(x_ref, wide, blocks)
    place_all(routes_ref, position_ref, blocks, out_ref, capacity)


def place_rows(routes, position, x, expert_count, capacity):
    tok_count, width = x.shape
    parts = width // LANES
    return pl.pallas_call(
        functools.partial(place_kernel, capacity),
        out_shape=jax.ShapeDtypeStruct((expert_count * capacity, parts, LANES), jnp.bfloat16),
        in_specs=[SMEM, SMEM, VMEM],
        out_specs=VMEM,
        scratch_shapes=[
            pltpu.VMEM((tok_count * parts, LANES), jnp.float32),
            pltpu.VMEM((tok_count, parts, LANES), jnp.bfloat16),
        ],
        compiler_params=params(),
        name="place_rows",
    )(routes, position, x)


def load_rows(x_ref, step, wide, rows_scr):
    rows = x_ref.shape[0]
    first = step * CHUNK
    wide[...] = x_ref[:, first : first + CHUNK, :].astype(jnp.float32).reshape(rows * CHUNK, LANES)
    for c in range(CHUNK):
        rows_scr[:, c * LANES : (c + 1) * LANES] = wide[pl.ds(c, rows, stride=CHUNK), :].astype(
            jnp.bfloat16
        )


def forward_kernel(x_ref, g0, g1, u0, u1, hidden_ref, slope_ref, active_ref, wide, rows_scr, acc_g, acc_u):
    step = pl.program_id(0)
    steps = x_ref.shape[1] // CHUNK

    @pl.when(step == 0)
    def _():
        acc_g[...] = jnp.zeros_like(acc_g)
        acc_u[...] = jnp.zeros_like(acc_u)

    for s in range(steps):

        @pl.when(step == s)
        def _():
            load_rows(x_ref, s, wide, rows_scr)

    rows = rows_scr[...]
    gate = jnp.concatenate([g0[...], g1[...]], axis=1)
    acc_g[...] += jnp.dot(rows, gate, preferred_element_type=jnp.float32)
    up = jnp.concatenate([u0[...], u1[...]], axis=1)
    acc_u[...] += jnp.dot(rows, up, preferred_element_type=jnp.float32)

    @pl.when(step == steps - 1)
    def _():
        gating = acc_g[...]
        lifted = acc_u[...]
        sigmoid = jax.nn.sigmoid(gating)
        active = gating * sigmoid
        hidden_ref[...] = (active * lifted).astype(jnp.bfloat16)
        slope_ref[...] = lifted * (sigmoid * (1.0 + gating * (1.0 - sigmoid)))
        active_ref[...] = active


def forward_terms(x, g0, g1, u0, u1):
    rows, parts, _ = x.shape
    half = g0.shape[1]
    hid = 2 * half
    depth = CHUNK * LANES
    weight = pl.BlockSpec((depth, half), lambda i: (i, 0))
    whole = pl.BlockSpec((rows, hid), lambda i: (0, 0))
    return pl.pallas_call(
        forward_kernel,
        grid=(parts // CHUNK,),
        out_shape=(
            jax.ShapeDtypeStruct((rows, hid), jnp.bfloat16),
            jax.ShapeDtypeStruct((rows, hid), jnp.float32),
            jax.ShapeDtypeStruct((rows, hid), jnp.float32),
        ),
        in_specs=[VMEM] + [weight] * 4,
        out_specs=(whole, whole, whole),
        scratch_shapes=[
            pltpu.VMEM((rows * CHUNK, LANES), jnp.float32),
            pltpu.VMEM((rows, depth), jnp.bfloat16),
            pltpu.VMEM((rows, hid), jnp.float32),
            pltpu.VMEM((rows, hid), jnp.float32),
        ],
        compiler_params=params(),
        name="forward_terms",
    )(on_chip(x), g0, g1, u0, u1)


def backward_kernel(
    x_ref, d0_hbm, d1_hbm, g0_hbm, g1_hbm, u0_hbm, u1_hbm, hidden_hbm, slope_hbm, active_hbm, out_ref,
    down, gate, up, hidden_ref, slope_ref, active_ref, grads, wide, column, stage, in_sems, out_sems,
):
    contract = (((1,), (1,)), ((), ()))
    rows, parts, _ = x_ref.shape
    steps = parts // CHUNK
    depth = CHUNK * LANES
    half = d0_hbm.shape[0]
    hid = 2 * half
    experts = out_ref.shape[0]
    capacity = rows // experts

    copies = []

    def fetch(src, dst):
        copy = pltpu.make_async_copy(src, dst, in_sems.at[len(copies)])
        copy.start()
        copies.append(copy)
        return copy

    down_in = []
    for step in range(steps):
        cols = pl.ds(step * depth, depth)
        down_in.append(
            [fetch(src.at[:, cols], down.at[step, pl.ds(h * half, half)]) for h, src in enumerate((d0_hbm, d1_hbm))]
        )
    terms_in = [
        fetch(hidden_hbm, hidden_ref), fetch(slope_hbm, slope_ref), fetch(active_hbm, active_ref)
    ]
    weights_in = []
    for step in range(steps):
        part = pl.ds(step * depth, depth)
        weights_in.append(
            [
                fetch(src.at[part], dst.at[h, part])
                for dst, pair in ((gate, (g0_hbm, g1_hbm)), (up, (u0_hbm, u1_hbm)))
                for h, src in enumerate(pair)
            ]
        )

    grad_hidden = None
    for step in range(steps):
        got = x_ref[:, step * CHUNK : (step + 1) * CHUNK, :].reshape(rows, depth)
        for copy in down_in[step]:
            copy.wait()
        total = lax.dot_general(got, down[step], contract, preferred_element_type=jnp.float32)
        grad_hidden = total if step == 0 else grad_hidden + total
    for copy in terms_in:
        copy.wait()
    grads[:, 0:hid] = (grad_hidden * slope_ref[...]).astype(jnp.bfloat16)
    grads[:, hid : 2 * hid] = (grad_hidden * active_ref[...]).astype(jnp.bfloat16)
    prob = jnp.sum(hidden_ref[...].astype(jnp.float32) * grad_hidden, axis=1, keepdims=True)
    column[...] = jnp.broadcast_to(prob, column.shape)
    wide[...] = jnp.zeros_like(wide)
    for s in range(capacity):
        wide[pl.ds(s, experts, stride=CHUNK), :] = column[pl.ds(s, experts, stride=capacity), :]
    stage[:, steps * capacity] = wide[...].reshape(experts, CHUNK, LANES).astype(jnp.bfloat16)

    sends = []

    def send(first, count):
        tiles = pl.ds(first, count)
        copy = pltpu.make_async_copy(
            stage.at[:, tiles], out_ref.at[:, tiles], out_sems.at[len(sends)]
        )
        copy.start()
        sends.append(copy)

    send(steps * capacity, 1)
    for step in range(steps):
        part = pl.ds(step * depth, depth)
        for copy in weights_in[step]:
            copy.wait()
        weight = jnp.concatenate([gate[0, part], gate[1, part], up[0, part], up[1, part]], axis=1)
        total = lax.dot_general(grads[...], weight, contract, preferred_element_type=jnp.float32)
        stage[:, step * capacity : (step + 1) * capacity] = total.astype(jnp.bfloat16).reshape(
            experts, capacity, CHUNK, LANES
        )
        send(step * capacity, capacity)
    for copy in sends:
        copy.wait()


def backward_terms(x, d0, d1, g0, g1, u0, u1, hidden, slope, active, expert_count):
    rows, parts, _ = x.shape
    width, half = g0.shape
    hid = 2 * half
    depth = CHUNK * LANES
    steps = parts // CHUNK
    tiles = rows // expert_count * steps + 1
    anywhere = pl.BlockSpec(memory_space=pl.ANY)
    return pl.pallas_call(
        backward_kernel,
        out_shape=jax.ShapeDtypeStruct((expert_count, tiles, CHUNK, LANES), jnp.bfloat16),
        in_specs=[VMEM] + [anywhere] * 9,
        out_specs=anywhere,
        scratch_shapes=[
            pltpu.VMEM((steps, hid, depth), jnp.bfloat16),
            pltpu.VMEM((2, width, half), jnp.bfloat16),
            pltpu.VMEM((2, width, half), jnp.bfloat16),
            pltpu.VMEM((rows, hid), jnp.bfloat16),
            pltpu.VMEM((rows, hid), jnp.float32),
            pltpu.VMEM((rows, hid), jnp.float32),
            pltpu.VMEM((rows, 2 * hid), jnp.bfloat16),
            pltpu.VMEM((expert_count * CHUNK, LANES), jnp.float32),
            pltpu.VMEM((rows, LANES), jnp.float32),
            pltpu.VMEM((expert_count, tiles, CHUNK, LANES), jnp.bfloat16),
            pltpu.SemaphoreType.DMA((6 * steps + 3,)),
            pltpu.SemaphoreType.DMA((steps + 1,)),
        ],
        compiler_params=params(),
        name="backward_terms",
    )(on_chip(x), d0, d1, g0, g1, u0, u1, hidden, slope, active)


def combine_kernel(capacity, routes_ref, position_ref, probs_ref, back_ref, out_ref, grad_ref, wide):
    top, tok_count = routes_ref.shape
    steps = (back_ref.shape[1] - 1) // capacity
    parts = steps * CHUNK
    sublane = lax.broadcasted_iota(jnp.int32, (CHUNK, LANES), 0)
    lane = lax.broadcasted_iota(jnp.int32, (CHUNK, LANES), 1)

    def gather(t, picked):
        chosen = [(routes_ref[k, t], position_ref[k, t], probs_ref[k, t]) for k in range(top)]
        for step in range(steps):
            total = jnp.zeros((CHUNK, LANES), jnp.float32)
            for e, position, prob in chosen:
                total += prob * back_ref[e, step * capacity + position].astype(jnp.float32)
            wide[pl.ds(pl.multiple_of(t * parts + step * CHUNK, CHUNK), CHUNK), :] = total
        new = []
        for k, (e, position, _) in enumerate(chosen):
            tile = back_ref[e, steps * capacity].astype(jnp.float32)
            here = (sublane == position) & (lane == t)
            new.append(picked[k] + jnp.where(here, tile, 0.0))
        return tuple(new)

    start = tuple(jnp.zeros((CHUNK, LANES), jnp.float32) for _ in range(top))
    picked = lax.fori_loop(0, tok_count, gather, start, unroll=4)
    for k in range(top):
        grad_ref[k : k + 1, :] = jnp.sum(picked[k], axis=0, keepdims=True)
    for c in range(parts):
        out_ref[:, c * LANES : (c + 1) * LANES] = wide[pl.ds(c, tok_count, stride=parts), :].astype(
            jnp.bfloat16
        )


def combine_rows(routes, position, probs, back, capacity):
    top, tok_count = routes.shape
    parts = (back.shape[1] - 1) // capacity * CHUNK
    return pl.pallas_call(
        functools.partial(combine_kernel, capacity),
        out_shape=(
            jax.ShapeDtypeStruct((tok_count, parts * LANES), jnp.bfloat16),
            jax.ShapeDtypeStruct((top, tok_count), jnp.float32),
        ),
        in_specs=[SMEM, SMEM, SMEM, VMEM],
        out_specs=(VMEM, VMEM),
        scratch_shapes=[pltpu.VMEM((tok_count * parts, LANES), jnp.float32)],
        compiler_params=params(),
        name="combine_rows",
    )(routes, position, probs, on_chip(back))


def exchange(blocks, expert_count):
    sent = blocks.reshape(expert_count, -1, blocks.shape[-1])
    got = lax.all_to_all(sent, "expert", split_axis=0, concat_axis=0, tiled=True)
    return got.reshape(blocks.shape)


def on_device(tokens, routes, route_probs, gate_weight, up_weight, down_weight, grad_out):
    tok_count = tokens.shape[0]
    top_count = routes.shape[1]
    expert_count = lax.axis_size("expert")
    capacity = 3 * tok_count * top_count // (2 * expert_count)
    swap = lambda w: lax.ppermute(w, "seq", [(0, 1), (1, 0)])
    gate, up, down = gate_weight[0], up_weight[0], down_weight[0]
    gate_far, up_far, down_far = swap(gate), swap(up), swap(down)
    named = routes.T

    position, send_in = route_and_place(named, tokens, expert_count, capacity)
    recv_in = exchange(send_in, expert_count)
    send_grad = place_rows(named, position, grad_out, expert_count, capacity)
    recv_grad = exchange(send_grad, expert_count)
    hidden, slope, active = forward_terms(recv_in, gate, gate_far, up, up_far)
    out_rows = backward_terms(
        recv_grad, down, down_far, gate, gate_far, up, up_far, hidden, slope, active, expert_count
    )
    back_rows = exchange(out_rows, expert_count)
    grad_tokens, grad_probs = combine_rows(named, position, route_probs.T, back_rows, capacity)
    return (grad_tokens, grad_probs.T.astype(jnp.bfloat16))


def solution(mesh):
    placed = (
        P(("seq", "expert"), None),
        P(("seq", "expert"), None),
        P(("seq", "expert"), None),
        P("expert", None, "seq"),
        P("expert", None, "seq"),
        P("expert", "seq", None),
        P(("seq", "expert"), None),
    )
    return jax.shard_map(
        on_device,
        mesh=mesh,
        in_specs=placed,
        out_specs=(P(("seq", "expert"), None), P(("seq", "expert"), None)),
        check_vma=False,
    )
```

time: 729 us -> 290 us (0.40)
  blocking collectives: 499 us -> 85 us
  local copies, waits for them, and re-layouts: 8.77 us -> 0 us
  other arithmetic: 9.62 us -> 1.16 us
    all_gather x1 -> x0, blocking collectives: 499 us -> none  [on_device(): all_prob = lax.all_gather(out_prob[:, 0], 'expert', axis=0, tiled=False)]
    all_to_all x0 -> x1, blocking collectives: none -> 85 us  [exchange(): lax.all_to_all(sent, 'expert', split_axis=0, concat_axis=0, tiled=True)]
    all_gather x1 -> x0, other arithmetic: 9.61 us -> none  [on_device(): all_prob = lax.all_gather(out_prob[:, 0], 'expert', axis=0, tiled=False)]
    all_to_all x3 -> x2, starting transfers between devices: 28.5 us -> 22.7 us  [exchange(): lax.all_to_all(sent, 'expert', split_axis=0, concat_axis=0, tiled=True)]
    all_to_all x3 -> x2, waiting for transfers between devices: 122 us -> 122 us  [exchange(): lax.all_to_all(sent, 'expert', split_axis=0, concat_axis=0, tiled=True)]
  transfers between devices with their start and end apart: 6 -> 5, of which waited for: 4 -> 4; matrix products, arithmetic and copies ran while one was open for 2% -> 0% of each run, Pallas kernels for 2% -> 6%
where the time goes in v2:
time: 290 us; the launch traced here: 289 us
  waiting for transfers between devices  132 us (46%)
  blocking collectives  85 us (29%)
  Pallas kernels  46.7 us (16%)
  starting transfers between devices  23.4 us (8%)
    all_to_all x2, waiting for transfers between devices, exchange(): lax.all_to_all(sent, 'expert', split_axis=0, concat_axis=0, tiled=True)  122 us
    all_to_all x1, blocking collectives, exchange(): lax.all_to_all(sent, 'expert', split_axis=0, concat_axis=0, tiled=True)  85 us
    all_to_all x2, starting transfers between devices, exchange(): lax.all_to_all(sent, 'expert', split_axis=0, concat_axis=0, tiled=True)  22.7 us
    pallas_call x1, Pallas kernels, backward_terms(): pl.pallas_call(backward_kernel, out_shape=jax.ShapeDtypeStruct((expert_co...  17.4 us
    pallas_call x1, Pallas kernels, forward_terms(): pl.pallas_call(forward_kernel, grid=(parts // CHUNK,), out_shape=(jax.Sha...  11.6 us
    ppermute x3, waiting for transfers between devices, on_device(): swap = lambda w: lax.ppermute(w, 'seq', [(0, 1), (1, 0)])  9.89 us
    pallas_call x1, Pallas kernels, route_and_place(): pl.pallas_call(functools.partial(route_kernel, capacity), out_shape=(jax....  7.27 us
    pallas_call x1, Pallas kernels, place_rows(): pl.pallas_call(functools.partial(place_kernel, capacity), out_shape=jax.S...  5.98 us
  transfers between devices with their start and end apart: 5, of which 4 were waited for; matrix products, arithmetic and copies ran while one was open for 0% of the time, Pallas kernels for 6%

profile of v2, /device:TPU:32, one launch (start us, length us, event | category | flops | bytes accessed | tf_op | source)
XLA Modules:
  0.0 289.1 jit_solution(3209568445142228537)
XLA Ops:
  0.6 7.3 %route_and_place.1 = (s32[2,128]{1,0:T(2,128)}, bf16[384,32,128]{2,1,0:T(8,128)(2,1)}) custom-call(s32[2,128]{1,0:T(2,128)} %bitcast.26, bf16[128,4096]{1,0:T(8,128)(2,1)} %x_ref.2), custom_call_target="tpu_custom_call" | custom-call | tf_op jit(solution)/shard_map/route_and_place/pallas_call | solution.py:79
  7.9 15.0 %all-to-all-start.1 = ((bf16[128,96,128]{2,1,0:T(8,128)(2,1)}), bf16[128,96,128]{2,1,0:T(8,128)(2,1)S(1)}, u32[]{:S(2)}, u32[]{:S(2)}) async-start(bf16[128,96,128]{2,1,0:T(8,128)(2,1)} %bitcast.25), calls=%async_computation.1 | async-start | bytes 6291456 | tf_op jit(solution)/shard_map/all_to_all | solution.py:355
  22.9 6.0 %place_rows.1 = bf16[384,32,128]{2,1,0:T(8,128)(2,1)} custom-call(s32[2,128]{1,0:T(2,128)} %bitcast.27, s32[2,128]{1,0:T(2,128)} %get-tuple-element.9.position_ref, bf16[128,4096]{1,0:T(8,128)(2,1)} %x_ref.3), custom_call_target="tpu_custom_call" | custom-call | tf_op jit(solution)/shard_map/place_rows/pallas_call | solution.py:105
  28.9 70.3 %all-to-all-done.1 = bf16[128,96,128]{2,1,0:T(8,128)(2,1)S(1)} async-done(((bf16[128,96,128]{2,1,0:T(8,128)(2,1)}), bf16[128,96,128]{2,1,0:T(8,128)(2,1)S(1)}, u32[]{:S(2)}, u32[]{:S(2)}) %all-to-all-start.1) | async-done | bytes 3145760 | tf_op jit(solution)/shard_map/all_to_all | solution.py:355
  99.2 7.7 %all-to-all-start = ((bf16[128,96,128]{2,1,0:T(8,128)(2,1)}), bf16[128,96,128]{2,1,0:T(8,128)(2,1)}, u32[]{:S(2)}, u32[]{:S(2)}) async-start(bf16[128,96,128]{2,1,0:T(8,128)(2,1)} %bitcast.16), calls=%async_computation | async-start | bytes 6291456 | tf_op jit(solution)/shard_map/all_to_all | solution.py:355
  106.9 0.1 collective-permute-start.1
  107.0 0.5 collective-permute-start.2
  107.5 0.1 collective-permute-start
  107.6 5.4 %collective-permute-done.1.g1.g1_hbm = bf16[4096,384]{1,0:T(8,128)(2,1)} collective-permute-done((bf16[4096,384]{1,0:T(8,128)(2,1)}, bf16[4096,384]{1,0:T(8,128)(2,1)}, u32[]{:S(2)}, u32[]{:S(2)}) %collective-permute-start.1) | collective-permute-done | bytes 3145760 | tf_op jit(solution)/shard_map/ppermute | solution.py:364
  113.0 4.5 %collective-permute-done.2.u1.u1_hbm = bf16[4096,384]{1,0:T(8,128)(2,1)} collective-permute-done((bf16[4096,384]{1,0:T(8,128)(2,1)}, bf16[4096,384]{1,0:T(8,128)(2,1)}, u32[]{:S(2)}, u32[]{:S(2)}) %collective-permute-start.2) | collective-permute-done | bytes 3145760 | tf_op jit(solution)/shard_map/ppermute | solution.py:364
  117.5 11.6 %forward_terms.1 = (bf16[384,768]{1,0:T(8,128)(2,1)}, f32[384,768]{1,0:T(8,128)}, f32[384,768]{1,0:T(8,128)}) custom-call(bf16[384,32,128]{2,1,0:T(8,128)(2,1)S(1)} %bitcast.14, bf16[4096,384]{1,0:T(8,128)(2,1)} %bitcast.18, bf16[4096,384]{1,0:T(8,128)(2,1)} %collective-permute-done.1.g1.g1_hbm, bf16[4096,384]{1,0:T(8,128)(2,1)} %bitcast.21, ...), custom_call_target="tpu_custom_call" | custom-call | tf_op jit(solution)/shard_map/forward_terms/pallas_call | solution.py:168
  129.1 0.0 collective-permute-done.d1_hbm
  129.1 52.0 %all-to-all-done = bf16[128,96,128]{2,1,0:T(8,128)(2,1)} async-done(((bf16[128,96,128]{2,1,0:T(8,128)(2,1)}), bf16[128,96,128]{2,1,0:T(8,128)(2,1)}, u32[]{:S(2)}, u32[]{:S(2)}) %all-to-all-start) | async-done | bytes 3145760 | tf_op jit(solution)/shard_map/all_to_all | solution.py:355
  181.1 17.4 %backward_terms.1 = bf16[128,13,8,128]{3,2,1,0:T(8,128)(2,1)} custom-call(bf16[384,32,128]{2,1,0:T(8,128)(2,1)} %bitcast.3.x_ref, bf16[384,4096]{1,0:T(8,128)(2,1)} %bitcast.24, bf16[384,4096]{1,0:T(8,128)(2,1)} %collective-permute-done.d1_hbm, bf16[4096,384]{1,0:T(8,128)(2,1)} %bitcast.19, bf16[4096,384]{1,0:T(8,128)(2,1)} %collective-permute-done.1.g1.g1_hbm, ...), custom_call_target="tpu_custom_call" | custom-call | tf_op jit(solution)/shard_map/backward_terms/pallas_call | solution.py:281
  198.5 85.0 %all_to_all.15 = bf16[128,104,128]{2,1,0:T(8,128)(2,1)S(1)} all-to-all(bf16[128,104,128]{2,1,0:T(8,128)(2,1)} %bitcast.15), channel_id=1, replica_groups=mesh['seq'=2,'expert'=128] {'expert'}, dimensions={0} | all-to-all | bytes 6815744 | tf_op jit(solution)/shard_map/all_to_all | solution.py:355
  283.5 4.4 %combine_rows.1 = (bf16[128,4096]{1,0:T(8,128)(2,1)}, f32[2,128]{1,0:T(2,128)}) custom-call(s32[2,128]{1,0:T(2,128)} %bitcast.28, s32[2,128]{1,0:T(2,128)} %get-tuple-element.9.position_ref, f32[2,128]{1,0:T(2,128)} %bitcast.29, bf16[128,13,8,128]{3,2,1,0:T(8,128)(2,1)S(1)} %bitcast.13), custom_call_target="tpu_custom_call" | custom-call | tf_op jit(solution)/shard_map/combine_rows/pallas_call | solution.py:339
  287.9 1.2 convert_bitcast_fusion
Async XLA Ops:
  7.9 91.3 %all-to-all-start.1 = ((bf16[128,96,128]{2,1,0:T(8,128)(2,1)}), bf16[128,96,128]{2,1,0:T(8,128)(2,1)S(1)}, u32[]{:S(2)}, u32[]{:S(2)}) async-start(bf16[128,96,128]{2,1,0:T(8,128)(2,1)} %bitcast.25), calls=%async_computation.1 | async-start | bytes 6291456 | tf_op jit(solution)/shard_map/all_to_all | solution.py:355
  99.2 81.9 %all-to-all-start = ((bf16[128,96,128]{2,1,0:T(8,128)(2,1)}), bf16[128,96,128]{2,1,0:T(8,128)(2,1)}, u32[]{:S(2)}, u32[]{:S(2)}) async-start(bf16[128,96,128]{2,1,0:T(8,128)(2,1)} %bitcast.16), calls=%async_computation | async-start | bytes 6291456 | tf_op jit(solution)/shard_map/all_to_all | solution.py:355
  106.9 6.1 %collective-permute-start.1 = (bf16[4096,384]{1,0:T(8,128)(2,1)}, bf16[4096,384]{1,0:T(8,128)(2,1)}, u32[]{:S(2)}, u32[]{:S(2)}) collective-permute-start(bf16[4096,384]{1,0:T(8,128)(2,1)} %bitcast.17), channel_id=1, source_target_pairs={{0,128},{128,0},{1,129},{129,1},{2,130},{130,2},{3,131},{131,3},{4... | collective-permute-start | bytes 9437192 | tf_op jit(solution)/shard_map/ppermute | solution.py:364
  107.0 10.5 %collective-permute-start.2 = (bf16[4096,384]{1,0:T(8,128)(2,1)}, bf16[4096,384]{1,0:T(8,128)(2,1)}, u32[]{:S(2)}, u32[]{:S(2)}) collective-permute-start(bf16[4096,384]{1,0:T(8,128)(2,1)} %bitcast.20), channel_id=1, source_target_pairs={{0,128},{128,0},{1,129},{129,1},{2,130},{130,2},{3,131},{131,3},{4... | collective-permute-start | bytes 9437192 | tf_op jit(solution)/shard_map/ppermute | solution.py:364
  107.5 21.6 %collective-permute-start = (bf16[384,4096]{1,0:T(8,128)(2,1)}, bf16[384,4096]{1,0:T(8,128)(2,1)}, u32[]{:S(2)}, u32[]{:S(2)}) collective-permute-start(bf16[384,4096]{1,0:T(8,128)(2,1)} %bitcast.23), channel_id=1, source_target_pairs={{0,128},{128,0},{1,129},{129,1},{2,130},{130,2},{3,131},{131,3},{4... | collective-permute-start | bytes 9437192 | tf_op jit(solution)/shard_map/ppermute | solution.py:364

commit v3 on v0

v3 whole, which is shorter than its diff:
```python
import functools

import jax
import jax.numpy as jnp
from jax import lax
from jax.experimental import pallas as pl
from jax.experimental.pallas import tpu as pltpu
from jax.sharding import PartitionSpec as P

LANES = 128
CHUNK = 8
GROUP = 16
MIB = 1024 * 1024
VMEM = pl.BlockSpec(memory_space=pltpu.VMEM)
SMEM = pl.BlockSpec(memory_space=pltpu.SMEM)
ANYWHERE = pl.BlockSpec(memory_space=pl.ANY)


def params(mib):
    return pltpu.CompilerParams(vmem_limit_bytes=mib * MIB)


def on_chip(x):
    return pltpu.with_memory_space_constraint(x, pltpu.VMEM)


def place_all(routes_ref, position_ref, rows_ref, blocks, stage):
    top, tok_count = routes_ref.shape
    capacity, parts = stage.shape[1:3]
    for r in range(0, tok_count, GROUP):
        blocks[r : r + GROUP] = rows_ref[r : r + GROUP, :].reshape(GROUP, parts, LANES)
    group = 8

    def place(g, _):
        first = g * group
        rows = [blocks[first + i] for i in range(group)]
        targets = [
            [(routes_ref[k, first + i], position_ref[k, first + i]) for k in range(top)]
            for i in range(group)
        ]
        for row, places in zip(rows, targets):
            for e, position in places:
                stage[e, position] = row
        return 0

    lax.fori_loop(0, tok_count // group, place, 0)


def pack_kernel(
    routes_ref, tokens_hbm, grads_hbm, position_ref, out_ref,
    counts, tokens_ref, grads_ref, blocks, stage_in, stage_grad, sems,
):
    top, tok_count = routes_ref.shape
    load_in = pltpu.make_async_copy(tokens_hbm, tokens_ref, sems.at[0])
    load_grad = pltpu.make_async_copy(grads_hbm, grads_ref, sems.at[1])
    load_in.start()
    load_grad.start()

    def clear(e, _):
        counts[e] = 0
        return 0

    lax.fori_loop(0, counts.shape[0], clear, 0, unroll=16)

    def rank(t, _):
        for k in range(top):
            e = routes_ref[k, t]
            position = counts[e]
            counts[e] = position + 1
            position_ref[k, t] = position
        return 0

    lax.fori_loop(0, tok_count, rank, 0, unroll=8)
    load_in.wait()
    place_all(routes_ref, position_ref, tokens_ref, blocks, stage_in)
    send_in = pltpu.make_async_copy(stage_in, out_ref.at[:, 0], sems.at[2])
    send_in.start()
    load_grad.wait()
    place_all(routes_ref, position_ref, grads_ref, blocks, stage_grad)
    send_grad = pltpu.make_async_copy(stage_grad, out_ref.at[:, 1], sems.at[3])
    send_grad.start()
    send_in.wait()
    send_grad.wait()


def pack(routes, tokens, grads, expert_count, capacity):
    tok_count, width = tokens.shape
    parts = width // LANES
    stage = pltpu.VMEM((expert_count, capacity, parts, LANES), jnp.bfloat16)
    return pl.pallas_call(
        pack_kernel,
        out_shape=(
            jax.ShapeDtypeStruct(routes.shape, jnp.int32),
            jax.ShapeDtypeStruct((expert_count, 2, capacity, parts, LANES), jnp.bfloat16),
        ),
        in_specs=[SMEM, ANYWHERE, ANYWHERE],
        out_specs=(SMEM, ANYWHERE),
        scratch_shapes=[
            pltpu.SMEM((expert_count,), jnp.int32),
            pltpu.VMEM((tok_count, width), jnp.bfloat16),
            pltpu.VMEM((tok_count, width), jnp.bfloat16),
            pltpu.VMEM((tok_count, parts, LANES), jnp.bfloat16),
            stage,
            stage,
            pltpu.SemaphoreType.DMA((4,)),
        ],
        compiler_params=params(62),
        name="pack",
    )(routes, tokens, grads)


def expert_kernel(
    x_hbm, d0_hbm, d1_hbm, g0_hbm, g1_hbm, u0_hbm, u1_hbm, out_ref,
    x_ref, down, gate_up, grads, wide, column, stage, in_sems, out_sems,
):
    contract = (((1,), (1,)), ((), ()))
    experts, _, capacity, parts, _ = x_hbm.shape
    rows = experts * capacity
    steps = parts // CHUNK
    depth = CHUNK * LANES
    half = d0_hbm.shape[0]
    hid = 2 * half

    fetches = []

    def fetch(src, dst):
        copy = pltpu.make_async_copy(src, dst, in_sems.at[len(fetches)])
        copy.start()
        fetches.append(copy)
        return copy

    def cut(step):
        return pl.ds(step * depth, depth)

    def fetch_rows(which, step):
        return fetch(
            x_hbm.at[:, which, :, pl.ds(step * CHUNK, CHUNK)], x_ref.at[which, step]
        )

    gate_up_in = [
        [fetch_rows(0, step)]
        + [
            fetch(src.at[cut(step)], gate_up.at[cut(step), pl.ds(h * half, half)])
            for h, src in enumerate((g0_hbm, g1_hbm, u0_hbm, u1_hbm))
        ]
        for step in range(steps)
    ]
    down_in = [
        [fetch_rows(1, step)]
        + [
            fetch(src.at[:, cut(step)], down.at[pl.ds(h * half, half), cut(step)])
            for h, src in enumerate((d0_hbm, d1_hbm))
        ]
        for step in range(steps)
    ]

    def taken(which, step):
        return x_ref[which, step].reshape(rows, CHUNK, LANES).reshape(rows, depth)

    both = None
    for step in range(steps):
        for copy in gate_up_in[step]:
            copy.wait()
        part = jnp.dot(taken(0, step), gate_up[cut(step)], preferred_element_type=jnp.float32)
        both = part if step == 0 else both + part
    wide[...] = both

    grad_hidden = None
    for step in range(steps):
        for copy in down_in[step]:
            copy.wait()
        part = lax.dot_general(
            taken(1, step), down[:, cut(step)], contract, preferred_element_type=jnp.float32
        )
        grad_hidden = part if step == 0 else grad_hidden + part

    gating = wide[:, 0:hid]
    lifted = wide[:, hid : 2 * hid]
    sigmoid = jax.nn.sigmoid(gating)
    active = gating * sigmoid
    hidden = (active * lifted).astype(jnp.bfloat16)
    slope = sigmoid * (1.0 + gating * (1.0 - sigmoid))
    grads[:, 0:hid] = (grad_hidden * lifted * slope).astype(jnp.bfloat16)
    grads[:, hid : 2 * hid] = (grad_hidden * active).astype(jnp.bfloat16)
    prob = jnp.sum(hidden.astype(jnp.float32) * grad_hidden, axis=1, keepdims=True)
    column[0:rows, :] = jnp.broadcast_to(prob, (rows, LANES))

    sends = []

    def send(tile):
        copy = pltpu.make_async_copy(stage.at[:, tile], out_ref.at[:, tile], out_sems.at[len(sends)])
        copy.start()
        sends.append(copy)

    for step in range(steps):
        part = lax.dot_general(
            grads[...], gate_up[cut(step)], contract, preferred_element_type=jnp.float32
        )
        tiles = part.astype(jnp.bfloat16).reshape(experts, capacity, CHUNK, LANES)
        for s in range(capacity):
            stage[:, s * steps + step] = tiles[:, s]
            send(s * steps + step)
        if step == 0:
            picked = [column[pl.ds(s, experts, stride=capacity), :] for s in range(capacity)]
            column[0 : experts * CHUNK, :] = jnp.zeros((experts * CHUNK, LANES), jnp.float32)
            for s in range(capacity):
                column[pl.ds(s, experts, stride=CHUNK), :] = picked[s]
            stage[:, capacity * steps] = (
                column[0 : experts * CHUNK, :].reshape(experts, CHUNK, LANES).astype(jnp.bfloat16)
            )
            send(capacity * steps)
    for copy in sends:
        copy.wait()


def expert_terms(x, d0, d1, g0, g1, u0, u1):
    expert_count, _, capacity, parts, _ = x.shape
    rows = expert_count * capacity
    width, half = g0.shape
    hid = 2 * half
    steps = parts // CHUNK
    tiles = capacity * steps + 1
    return pl.pallas_call(
        expert_kernel,
        out_shape=jax.ShapeDtypeStruct((expert_count, tiles, CHUNK, LANES), jnp.bfloat16),
        in_specs=[ANYWHERE] * 7,
        out_specs=ANYWHERE,
        scratch_shapes=[
            pltpu.VMEM((2, steps, expert_count, capacity, CHUNK, LANES), jnp.bfloat16),
            pltpu.VMEM((hid, width), jnp.bfloat16),
            pltpu.VMEM((width, 2 * hid), jnp.bfloat16),
            pltpu.VMEM((rows, 2 * hid), jnp.bfloat16),
            pltpu.VMEM((rows, 2 * hid), jnp.float32),
            pltpu.VMEM((max(rows, expert_count * CHUNK), LANES), jnp.float32),
            pltpu.VMEM((expert_count, tiles, CHUNK, LANES), jnp.bfloat16),
            pltpu.SemaphoreType.DMA((8 * steps,)),
            pltpu.SemaphoreType.DMA((tiles,)),
        ],
        compiler_params=params(62),
        name="expert_terms",
    )(x, d0, d1, g0, g1, u0, u1)


def combine_kernel(routes_ref, position_ref, probs_ref, back_ref, out_ref, grad_ref, blocks):
    top, tok_count = routes_ref.shape
    parts = blocks.shape[1]
    steps = parts // CHUNK
    last = back_ref.shape[1] - 1
    group = 4
    sublane = lax.broadcasted_iota(jnp.int32, (CHUNK, LANES), 0)
    lane = lax.broadcasted_iota(jnp.int32, (CHUNK, LANES), 1)

    def gather(g, picked):
        picked = list(picked)
        rows = []
        for i in range(group):
            t = g * group + i
            total = None
            for k in range(top):
                e, position = routes_ref[k, t], position_ref[k, t]
                row = back_ref[e, pl.ds(position * steps, steps)].reshape(parts, LANES)
                term = probs_ref[k, t] * row.astype(jnp.float32)
                total = term if k == 0 else total + term
                tile = back_ref[e, last].astype(jnp.float32)
                here = (sublane == position) & (lane == t)
                picked[k] = jnp.where(here, tile, picked[k])
            rows.append(total.astype(jnp.bfloat16))
        for i in range(group):
            blocks[g * group + i] = rows[i]
        return tuple(picked)

    start = tuple(jnp.zeros((CHUNK, LANES), jnp.float32) for _ in range(top))
    picked = lax.fori_loop(0, tok_count // group, gather, start)
    grad_ref[...] = jnp.concatenate(
        [jnp.sum(p, axis=0, keepdims=True) for p in picked], axis=0
    ).astype(jnp.bfloat16)
    for r in range(0, tok_count, GROUP):
        out_ref[r : r + GROUP, :] = blocks[r : r + GROUP].reshape(GROUP, parts * LANES)


def combine(routes, position, probs, back, width):
    top, tok_count = routes.shape
    return pl.pallas_call(
        combine_kernel,
        out_shape=(
            jax.ShapeDtypeStruct((tok_count, width), jnp.bfloat16),
            jax.ShapeDtypeStruct((top, tok_count), jnp.bfloat16),
        ),
        in_specs=[SMEM, SMEM, SMEM, VMEM],
        out_specs=(VMEM, VMEM),
        scratch_shapes=[pltpu.VMEM((tok_count, width // LANES, LANES), jnp.bfloat16)],
        compiler_params=params(56),
        name="combine",
    )(routes, position, probs, on_chip(back))


def exchange(blocks):
    sent = blocks.reshape(blocks.shape[0], -1, blocks.shape[-1])
    got = lax.all_to_all(sent, "expert", split_axis=0, concat_axis=0, tiled=True)
    return got.reshape(blocks.shape)


def on_device(tokens, routes, route_probs, gate_weight, up_weight, down_weight, grad_out):
    tok_count, width = tokens.shape
    top_count = routes.shape[1]
    expert_count = lax.axis_size("expert")
    capacity = 3 * tok_count * top_count // (2 * expert_count)
    swap = lambda w: lax.ppermute(w, "seq", [(0, 1), (1, 0)])
    gate, up, down = gate_weight[0], up_weight[0], down_weight[0]
    gate_far, up_far, down_far = swap(gate), swap(up), swap(down)
    named = routes.T

    position, sent = pack(named, tokens, grad_out, expert_count, capacity)
    received = exchange(sent)
    rows = expert_terms(received, down, down_far, gate, gate_far, up, up_far)
    back = exchange(rows)
    grad_tokens, grad_probs = combine(named, position, route_probs.T, back, width)
    return (grad_tokens, grad_probs.T)


def solution(mesh):
    placed = (
        P(("seq", "expert"), None),
        P(("seq", "expert"), None),
        P(("seq", "expert"), None),
        P("expert", None, "seq"),
        P("expert", None, "seq"),
        P("expert", "seq", None),
        P(("seq", "expert"), None),
    )
    return jax.shard_map(
        on_device,
        mesh=mesh,
        in_specs=placed,
        out_specs=(P(("seq", "expert"), None), P(("seq", "expert"), None)),
        check_vma=False,
    )
```

time: 586 us -> 277 us (0.47); the launches traced: 575 us -> 276 us
  local copies, waits for them, and re-layouts: 145 us -> 3.3 us
  blocking collectives: 218 us -> 86 us
  matrix products: 36.7 us -> 0 us
  Pallas kernels: 0 us -> 30.4 us
  between operations: 15.1 us -> 0.68 us
  other arithmetic: 11 us -> 0 us
  waiting for transfers between devices: 129 us -> 139 us
    all_to_all x2 -> x1, blocking collectives: 218 us -> 86 us  [exchange(): lax.all_to_all(sent, 'expert', split_axis=0, concat_axis=0, tiled=True)]
    reshape x7 -> x0, local copies, waits for them, and re-layouts: 50.1 us -> none  [the longest x1 14.1 us: on_device(): both_in.reshape(-1, model_width)]
    dot_general x5 -> x0, matrix products: 36.7 us -> none  [the longest x1 12.4 us: expert_terms(): lax.dot_general(grad_up, up_w, contract, preferred_element_type=jnp.float32)]
    unnamed x5 -> x0, waiting for transfers between devices: 33.1 us -> none
    all_to_all x2 -> x1, waiting for transfers between devices: 95.6 us -> 127 us  [exchange(): lax.all_to_all(sent, 'expert', split_axis=0, concat_axis=0, tiled=True)]
    pallas_call x0 -> x3, Pallas kernels: none -> 30.4 us  [the longest x1 20.5 us: expert_terms(): pl.pallas_call(expert_kernel, out_shape=jax.ShapeDtypeStruct((expert_coun...]
    all_gather x2 -> x0, local copies, waits for them, and re-layouts: 23.8 us -> none  [the longest x1 12.4 us: on_device(): lax.all_gather(recv_in, 'seq', axis=0, tiled=True)]
    scatter x2 -> x0, local copies, waits for them, and re-layouts: 21.8 us -> none  [the longest x1 11 us: on_device(): blank_rows.at[slot_ids].set(tokens[source])]
  transfers between devices with their start and end apart: 6 -> 4, of which waited for: 2 -> 3; matrix products, arithmetic and copies ran while one was open for 17% -> 0% of each run, Pallas kernels for 0% -> 0%
where the time goes in v3:
time: 277 us; the launch traced here: 276 us
  waiting for transfers between devices  139 us (50%)
  blocking collectives  86 us (31%)
  Pallas kernels  30.4 us (11%)
  starting transfers between devices  16.4 us (6%)
  local copies, waits for them, and re-layouts  3.3 us (1%)
    all_to_all x1, waiting for transfers between devices, exchange(): lax.all_to_all(sent, 'expert', split_axis=0, concat_axis=0, tiled=True)  127 us
    all_to_all x1, blocking collectives, exchange(): lax.all_to_all(sent, 'expert', split_axis=0, concat_axis=0, tiled=True)  86 us
    pallas_call x1, Pallas kernels, expert_terms(): pl.pallas_call(expert_kernel, out_shape=jax.ShapeDtypeStruct((expert_coun...  20.5 us
    all_to_all x1, starting transfers between devices, exchange(): lax.all_to_all(sent, 'expert', split_axis=0, concat_axis=0, tiled=True)  15.7 us
    ppermute x3, waiting for transfers between devices, on_device(): swap = lambda w: lax.ppermute(w, 'seq', [(0, 1), (1, 0)])  12.3 us
    pallas_call x1, Pallas kernels, pack(): pl.pallas_call(pack_kernel, out_shape=(jax.ShapeDtypeStruct(routes.shape,...  6.77 us
  transfers between devices with their start and end apart: 4, of which 3 were waited for; matrix products, arithmetic and copies ran while one was open for 0% of the time, Pallas kernels for 0%

profile of v3, /device:TPU:32, one launch (start us, length us, event | category | flops | bytes accessed | tf_op | source)
XLA Modules:
  0.0 276.2 jit_solution(3590718683792239535)
XLA Ops:
  0.6 6.8 %pack.1 = (s32[2,128]{1,0:T(2,128)}, bf16[128,2,3,32,128]{4,3,2,1,0:T(8,128)(2,1)}) custom-call(s32[2,128]{1,0:T(2,128)} %bitcast.19, bf16[128,4096]{1,0:T(8,128)(2,1)} %tokens_hbm.1, bf16[128,4096]{1,0:T(8,128)(2,1)} %grads_hbm.1), custom_call_target="tpu_custom_call" | custom-call | tf_op jit(solution)/shard_map/pack/pallas_call | solution.py:90
  7.4 0.0 copy-start
  7.4 15.7 %all-to-all-start = ((bf16[128,192,128]{2,1,0:T(8,128)(2,1)}), bf16[128,192,128]{2,1,0:T(8,128)(2,1)}, u32[]{:S(2)}, u32[]{:S(2)}) async-start(bf16[128,192,128]{2,1,0:T(8,128)(2,1)} %bitcast.12), calls=%async_computation | async-start | bytes 12582912 | tf_op jit(solution)/shard_map/all_to_all | solution.py:299
  23.1 0.0 copy-done
  23.1 0.1 collective-permute-start
  23.2 0.5 collective-permute-start.1
  23.7 0.1 collective-permute-start.2
  23.8 8.5 %collective-permute-done.d1_hbm = bf16[384,4096]{1,0:T(8,128)(2,1)S(1)} collective-permute-done((bf16[384,4096]{1,0:T(8,128)(2,1)S(1)}, bf16[384,4096]{1,0:T(8,128)(2,1)S(1)}, u32[]{:S(2)}, u32[]{:S(2)}) %collective-permute-start) | collective-permute-done | bytes 3145760 | tf_op jit(solution)/shard_map/ppermute | solution.py:308
  32.4 0.0 copy-start.1
  32.4 1.6 copy-done.1
  34.0 3.7 %collective-permute-done.1.g1_hbm = bf16[4096,384]{1,0:T(8,128)(2,1)S(1)} collective-permute-done((bf16[4096,384]{1,0:T(8,128)(2,1)}, bf16[4096,384]{1,0:T(8,128)(2,1)S(1)}, u32[]{:S(2)}, u32[]{:S(2)}) %collective-permute-start.1) | collective-permute-done | bytes 3145760 | tf_op jit(solution)/shard_map/ppermute | solution.py:308
  37.7 0.0 copy-start.2
  37.7 1.7 copy-done.2
  39.4 0.0 collective-permute-done.2.u1_hbm
  39.4 127.2 %all-to-all-done = bf16[128,192,128]{2,1,0:T(8,128)(2,1)} async-done(((bf16[128,192,128]{2,1,0:T(8,128)(2,1)}), bf16[128,192,128]{2,1,0:T(8,128)(2,1)}, u32[]{:S(2)}, u32[]{:S(2)}) %all-to-all-start) | async-done | bytes 6291488 | tf_op jit(solution)/shard_map/all_to_all | solution.py:299
  166.5 20.5 %expert_terms.1 = bf16[128,13,8,128]{3,2,1,0:T(8,128)(2,1)} custom-call(bf16[128,2,3,32,128]{4,3,2,1,0:T(8,128)(2,1)} %bitcast.3.x_hbm, bf16[384,4096]{1,0:T(8,128)(2,1)} %bitcast.13, bf16[384,4096]{1,0:T(8,128)(2,1)} %copy-done.1, bf16[4096,384]{1,0:T(8,128)(2,1)} %bitcast.16, bf16[4096,384]{1,0:T(8,128)(2,1)} %copy-done.2, bf16[4096,384]{1,0:T(8,128)(2,1)} %bitcast.18, ...), custom_call_target="tpu_custom_call" | custom-call | tf_op jit(solution)/shard_map/expert_terms/pallas_call | solution.py:223
  187.0 86.0 %all_to_all.10 = bf16[128,104,128]{2,1,0:T(8,128)(2,1)S(1)} all-to-all(bf16[128,104,128]{2,1,0:T(8,128)(2,1)} %bitcast.11), channel_id=1, replica_groups=mesh['seq'=2,'expert'=128] {'expert'}, dimensions={0} | all-to-all | bytes 6815744 | tf_op jit(solution)/shard_map/all_to_all | solution.py:299
  273.0 3.2 %combine.1 = (bf16[128,4096]{1,0:T(8,128)(2,1)}, bf16[2,128]{1,0:T(2,128)(2,1)}) custom-call(s32[2,128]{1,0:T(2,128)} %bitcast.20, s32[2,128]{1,0:T(2,128)} %get-tuple-element.6.position_ref, f32[2,128]{1,0:T(2,128)} %bitcast.21, bf16[128,13,8,128]{3,2,1,0:T(8,128)(2,1)S(1)} %bitcast.10), custom_call_target="tpu_custom_call" | custom-call | tf_op jit(solution)/shard_map/combine/pallas_call | solution.py:283
Async XLA Ops:
  7.4 15.7 %copy-start = (bf16[1,384,4096]{2,1,0:T(8,128)(2,1)S(1)}, bf16[1,384,4096]{2,1,0:T(8,128)(2,1)}, u32[]{:S(2)}) copy-start(bf16[1,384,4096]{2,1,0:T(8,128)(2,1)} %param.12) | copy-start | bytes 9437188
  7.4 159.1 %all-to-all-start = ((bf16[128,192,128]{2,1,0:T(8,128)(2,1)}), bf16[128,192,128]{2,1,0:T(8,128)(2,1)}, u32[]{:S(2)}, u32[]{:S(2)}) async-start(bf16[128,192,128]{2,1,0:T(8,128)(2,1)} %bitcast.12), calls=%async_computation | async-start | bytes 12582912 | tf_op jit(solution)/shard_map/all_to_all | solution.py:299
  23.1 9.2 %collective-permute-start = (bf16[384,4096]{1,0:T(8,128)(2,1)S(1)}, bf16[384,4096]{1,0:T(8,128)(2,1)S(1)}, u32[]{:S(2)}, u32[]{:S(2)}) collective-permute-start(bf16[384,4096]{1,0:T(8,128)(2,1)S(1)} %bitcast.14), channel_id=1, source_target_pairs={{0,128},{128,0},{1,129},{129,1},{2,130},{130,2},{3,131},{131,3},{4... | collective-permute-start | bytes 9437192 | tf_op jit(solution)/shard_map/ppermute | solution.py:308
  23.2 14.5 %collective-permute-start.1 = (bf16[4096,384]{1,0:T(8,128)(2,1)}, bf16[4096,384]{1,0:T(8,128)(2,1)S(1)}, u32[]{:S(2)}, u32[]{:S(2)}) collective-permute-start(bf16[4096,384]{1,0:T(8,128)(2,1)} %bitcast.15), channel_id=1, source_target_pairs={{0,128},{128,0},{1,129},{129,1},{2,130},{130,2},{3,131},{131,3},{4... | collective-permute-start | bytes 9437192 | tf_op jit(solution)/shard_map/ppermute | solution.py:308
  23.7 15.7 %collective-permute-start.2 = (bf16[4096,384]{1,0:T(8,128)(2,1)}, bf16[4096,384]{1,0:T(8,128)(2,1)}, u32[]{:S(2)}, u32[]{:S(2)}) collective-permute-start(bf16[4096,384]{1,0:T(8,128)(2,1)} %bitcast.17), channel_id=1, source_target_pairs={{0,128},{128,0},{1,129},{129,1},{2,130},{130,2},{3,131},{131,3},{4... | collective-permute-start | bytes 9437192 | tf_op jit(solution)/shard_map/ppermute | solution.py:308
  32.4 1.6 copy-start.1
  37.7 1.7 copy-start.2

commit v4 on v3

--- a/solution.py
+++ b/solution.py
@@ -10,6 +10,8 @@
 LANES = 128
 CHUNK = 8
 GROUP = 16
+AHEAD = 8
+BLOCKS = 1
 MIB = 1024 * 1024
 VMEM = pl.BlockSpec(memory_space=pltpu.VMEM)
 SMEM = pl.BlockSpec(memory_space=pltpu.SMEM)
@@ -24,33 +26,26 @@
     return pltpu.with_memory_space_constraint(x, pltpu.VMEM)
 
 
-def place_all(routes_ref, position_ref, rows_ref, blocks, stage):
-    top, tok_count = routes_ref.shape
-    capacity, parts = stage.shape[1:3]
-    for r in range(0, tok_count, GROUP):
-        blocks[r : r + GROUP] = rows_ref[r : r + GROUP, :].reshape(GROUP, parts, LANES)
-    group = 8
+def place_rows(rows_ref, stage, slots_of):
+    tok_count = rows_ref.shape[0]
+    parts = stage.shape[2]
 
     def place(g, _):
-        first = g * group
-        rows = [blocks[first + i] for i in range(group)]
-        targets = [
-            [(routes_ref[k, first + i], position_ref[k, first + i]) for k in range(top)]
-            for i in range(group)
-        ]
-        for row, places in zip(rows, targets):
-            for e, position in places:
-                stage[e, position] = row
+        first = pl.multiple_of(g * GROUP, GROUP)
+        rows = rows_ref[pl.ds(first, GROUP), :].reshape(GROUP, parts, LANES)
+        for i in range(GROUP):
+            for e, position in slots_of(first + i):
+                stage[e, position] = rows[i]
         return 0
 
-    lax.fori_loop(0, tok_count // group, place, 0)
+    lax.fori_loop(0, tok_count // GROUP, place, 0)
 
 
 def pack_kernel(
     routes_ref, tokens_hbm, grads_hbm, position_ref, out_ref,
-    counts, tokens_ref, grads_ref, blocks, stage_in, stage_grad, sems,
+    counts, tokens_ref, grads_ref, stage_in, stage_grad, sems,
 ):
-    top, tok_count = routes_ref.shape
+    top = routes_ref.shape[0]
     load_in = pltpu.make_async_copy(tokens_hbm, tokens_ref, sems.at[0])
     load_grad = pltpu.make_async_copy(grads_hbm, grads_ref, sems.at[1])
     load_in.start()
@@ -62,21 +57,25 @@
 
     lax.fori_loop(0, counts.shape[0], clear, 0, unroll=16)
 
-    def rank(t, _):
+    def ranked(t):
+        slots = []
         for k in range(top):
             e = routes_ref[k, t]
             position = counts[e]
             counts[e] = position + 1
             position_ref[k, t] = position
-        return 0
-
-    lax.fori_loop(0, tok_count, rank, 0, unroll=8)
+            slots.append((e, position))
+        return slots
+
+    def known(t):
+        return [(routes_ref[k, t], position_ref[k, t]) for k in range(top)]
+
     load_in.wait()
-    place_all(routes_ref, position_ref, tokens_ref, blocks, stage_in)
+    place_rows(tokens_ref, stage_in, ranked)
     send_in = pltpu.make_async_copy(stage_in, out_ref.at[:, 0], sems.at[2])
     send_in.start()
     load_grad.wait()
-    place_all(routes_ref, position_ref, grads_ref, blocks, stage_grad)
+    place_rows(grads_ref, stage_grad, known)
     send_grad = pltpu.make_async_copy(stage_grad, out_ref.at[:, 1], sems.at[3])
     send_grad.start()
     send_in.wait()
@@ -99,7 +98,6 @@
             pltpu.SMEM((expert_count,), jnp.int32),
             pltpu.VMEM((tok_count, width), jnp.bfloat16),
             pltpu.VMEM((tok_count, width), jnp.bfloat16),
-            pltpu.VMEM((tok_count, parts, LANES), jnp.bfloat16),
             stage,
             stage,
             pltpu.SemaphoreType.DMA((4,)),
@@ -120,32 +118,29 @@
     depth = CHUNK * LANES
     half = d0_hbm.shape[0]
     hid = 2 * half
-
-    fetches = []
-
-    def fetch(src, dst):
-        copy = pltpu.make_async_copy(src, dst, in_sems.at[len(fetches)])
-        copy.start()
-        fetches.append(copy)
-        return copy
+    dests = experts // BLOCKS
+    some = dests * capacity
 
     def cut(step):
         return pl.ds(step * depth, depth)
 
+    count = [0]
+
+    def fetch(src, dst):
+        count[0] += 1
+        return pltpu.make_async_copy(src, dst, in_sems.at[count[0] - 1])
+
     def fetch_rows(which, step):
-        return fetch(
-            x_hbm.at[:, which, :, pl.ds(step * CHUNK, CHUNK)], x_ref.at[which, step]
-        )
-
-    gate_up_in = [
+        return fetch(x_hbm.at[:, which, :, pl.ds(step * CHUNK, CHUNK)], x_ref.at[which, step])
+
+    batches = [
         [fetch_rows(0, step)]
         + [
             fetch(src.at[cut(step)], gate_up.at[cut(step), pl.ds(h * half, half)])
             for h, src in enumerate((g0_hbm, g1_hbm, u0_hbm, u1_hbm))
         ]
         for step in range(steps)
-    ]
-    down_in = [
+    ] + [
         [fetch_rows(1, step)]
         + [
             fetch(src.at[:, cut(step)], down.at[pl.ds(h * half, half), cut(step)])
@@ -153,62 +148,86 @@
         ]
         for step in range(steps)
     ]
-
-    def taken(which, step):
-        return x_ref[which, step].reshape(rows, CHUNK, LANES).reshape(rows, depth)
+    for batch in batches[:AHEAD]:
+        for copy in batch:
+            copy.start()
+
+    def arrive(i):
+        for copy in batches[i]:
+            copy.wait()
+        for batch in batches[i + AHEAD : i + AHEAD + 1]:
+            for copy in batch:
+                copy.start()
+
+    def taken(which, step, first, number):
+        part = x_ref[which, step, first : first + number]
+        return part.reshape(number * capacity, CHUNK, LANES).reshape(number * capacity, depth)
 
     both = None
     for step in range(steps):
-        for copy in gate_up_in[step]:
-            copy.wait()
-        part = jnp.dot(taken(0, step), gate_up[cut(step)], preferred_element_type=jnp.float32)
+        arrive(step)
+        part = jnp.dot(
+            taken(0, step, 0, experts), gate_up[cut(step)], preferred_element_type=jnp.float32
+        )
         both = part if step == 0 else both + part
     wide[...] = both
-
-    grad_hidden = None
     for step in range(steps):
-        for copy in down_in[step]:
-            copy.wait()
-        part = lax.dot_general(
-            taken(1, step), down[:, cut(step)], contract, preferred_element_type=jnp.float32
+        arrive(steps + step)
+
+    for b in range(BLOCKS):
+        here = slice(b * some, (b + 1) * some)
+        grad_hidden = None
+        for step in range(steps):
+            part = lax.dot_general(
+                taken(1, step, b * dests, dests),
+                down[:, cut(step)],
+                contract,
+                preferred_element_type=jnp.float32,
+            )
+            grad_hidden = part if step == 0 else grad_hidden + part
+        gating = wide[here, 0:hid]
+        lifted = wide[here, hid : 2 * hid]
+        sigmoid = jax.nn.sigmoid(gating)
+        active = gating * sigmoid
+        hidden = (active * lifted).astype(jnp.bfloat16)
+        slope = sigmoid * (1.0 + gating * (1.0 - sigmoid))
+        grads[here, 0:hid] = (grad_hidden * lifted * slope).astype(jnp.bfloat16)
+        grads[here, hid : 2 * hid] = (grad_hidden * active).astype(jnp.bfloat16)
+        prob = jnp.sum(hidden.astype(jnp.float32) * grad_hidden, axis=1, keepdims=True)
+        column[here, :] = jnp.broadcast_to(prob, (some, LANES))
+
+    sends = []
+
+    def send(first, number, tile):
+        places = pl.ds(first, number)
+        copy = pltpu.make_async_copy(
+            stage.at[places, tile], out_ref.at[places, tile], out_sems.at[len(sends)]
         )
-        grad_hidden = part if step == 0 else grad_hidden + part
-
-    gating = wide[:, 0:hid]
-    lifted = wide[:, hid : 2 * hid]
-    sigmoid = jax.nn.sigmoid(gating)
-    active = gating * sigmoid
-    hidden = (active * lifted).astype(jnp.bfloat16)
-    slope = sigmoid * (1.0 + gating * (1.0 - sigmoid))
-    grads[:, 0:hid] = (grad_hidden * lifted * slope).astype(jnp.bfloat16)
-    grads[:, hid : 2 * hid] = (grad_hidden * active).astype(jnp.bfloat16)
-    prob = jnp.sum(hidden.astype(jnp.float32) * grad_hidden, axis=1, keepdims=True)
-    column[0:rows, :] = jnp.broadcast_to(prob, (rows, LANES))
-
-    sends = []
-
-    def send(tile):
-        copy = pltpu.make_async_copy(stage.at[:, tile], out_ref.at[:, tile], out_sems.at[len(sends)])
         copy.start()
         sends.append(copy)
 
-    for step in range(steps):
-        part = lax.dot_general(
-            grads[...], gate_up[cut(step)], contract, preferred_element_type=jnp.float32
-        )
-        tiles = part.astype(jnp.bfloat16).reshape(experts, capacity, CHUNK, LANES)
-        for s in range(capacity):
-            stage[:, s * steps + step] = tiles[:, s]
-            send(s * steps + step)
-        if step == 0:
-            picked = [column[pl.ds(s, experts, stride=capacity), :] for s in range(capacity)]
-            column[0 : experts * CHUNK, :] = jnp.zeros((experts * CHUNK, LANES), jnp.float32)
+    for b in range(BLOCKS):
+        for step in range(steps):
+            part = lax.dot_general(
+                grads[b * some : (b + 1) * some, :],
+                gate_up[cut(step)],
+                contract,
+                preferred_element_type=jnp.float32,
+            )
+            tiles = part.astype(jnp.bfloat16).reshape(dests, capacity, CHUNK, LANES)
             for s in range(capacity):
-                column[pl.ds(s, experts, stride=CHUNK), :] = picked[s]
-            stage[:, capacity * steps] = (
-                column[0 : experts * CHUNK, :].reshape(experts, CHUNK, LANES).astype(jnp.bfloat16)
-            )
-            send(capacity * steps)
+                stage[b * dests : (b + 1) * dests, s * steps + step] = tiles[:, s]
+            if b == 0 and step == 0:
+                picked = [column[pl.ds(s, experts, stride=capacity), :] for s in range(capacity)]
+                column[0 : experts * CHUNK, :] = jnp.zeros((experts * CHUNK, LANES), jnp.float32)
+                for s in range(capacity):
+                    column[pl.ds(s, experts, stride=CHUNK), :] = picked[s]
+                stage[:, capacity * steps] = (
+                    column[0 : experts * CHUNK, :].reshape(experts, CHUNK, LANES).astype(jnp.bfloat16)
+                )
+                send(0, experts, capacity * steps)
+            for s in range(capacity):
+                send(b * dests, dests, s * steps + step)
     for copy in sends:
         copy.wait()
 
@@ -234,9 +253,9 @@
             pltpu.VMEM((max(rows, expert_count * CHUNK), LANES), jnp.float32),
             pltpu.VMEM((expert_count, tiles, CHUNK, LANES), jnp.bfloat16),
             pltpu.SemaphoreType.DMA((8 * steps,)),
-            pltpu.SemaphoreType.DMA((tiles,)),
+            pltpu.SemaphoreType.DMA((BLOCKS * (tiles - 1) + 1,)),
         ],
-        compiler_params=params(62),
+        compiler_params=params(50),
         name="expert_terms",
     )(x, d0, d1, g0, g1, u0, u1)
 

time: 277 us -> 275 us (level)
  no operation moved by 1% of the time
where the time goes in v4:
time: 275 us
  waiting for transfers between devices  139 us (51%)
  blocking collectives  86.1 us (31%)
  Pallas kernels  29.3 us (11%)
  starting transfers between devices  16.4 us (6%)
  local copies, waits for them, and re-layouts  3.3 us (1%)
    all_to_all x1, waiting for transfers between devices, exchange(): lax.all_to_all(sent, 'expert', split_axis=0, concat_axis=0, tiled=True)  127 us
    all_to_all x1, blocking collectives, exchange(): lax.all_to_all(sent, 'expert', split_axis=0, concat_axis=0, tiled=True)  86.1 us
    pallas_call x1, Pallas kernels, expert_terms(): pl.pallas_call(expert_kernel, out_shape=jax.ShapeDtypeStruct((expert_coun...  19.4 us
    all_to_all x1, starting transfers between devices, exchange(): lax.all_to_all(sent, 'expert', split_axis=0, concat_axis=0, tiled=True)  15.7 us
    ppermute x3, waiting for transfers between devices, on_device(): swap = lambda w: lax.ppermute(w, 'seq', [(0, 1), (1, 0)])  12.3 us
    pallas_call x1, Pallas kernels, pack(): pl.pallas_call(pack_kernel, out_shape=(jax.ShapeDtypeStruct(routes.shape,...  6.7 us
  transfers between devices with their start and end apart: 4, of which 3 were waited for; matrix products, arithmetic and copies ran while one was open for 0% of the time, Pallas kernels for 0%

profile of v4, /device:TPU:32, one launch (start us, length us, event | category | flops | bytes accessed | tf_op | source)
XLA Modules:
  0.0 275.1 jit_solution(2049438360265792920)
XLA Ops:
  0.6 6.7 %pack.1 = (s32[2,128]{1,0:T(2,128)}, bf16[128,2,3,32,128]{4,3,2,1,0:T(8,128)(2,1)}) custom-call(s32[2,128]{1,0:T(2,128)} %bitcast.19, bf16[128,4096]{1,0:T(8,128)(2,1)} %tokens_hbm.1, bf16[128,4096]{1,0:T(8,128)(2,1)} %grads_hbm.1), custom_call_target="tpu_custom_call" | custom-call | tf_op jit(solution)/shard_map/pack/pallas_call | solution.py:89
  7.3 0.0 copy-start
  7.3 15.7 %all-to-all-start = ((bf16[128,192,128]{2,1,0:T(8,128)(2,1)}), bf16[128,192,128]{2,1,0:T(8,128)(2,1)}, u32[]{:S(2)}, u32[]{:S(2)}) async-start(bf16[128,192,128]{2,1,0:T(8,128)(2,1)} %bitcast.14), calls=%async_computation | async-start | bytes 12582912 | tf_op jit(solution)/shard_map/all_to_all | solution.py:318
  23.0 0.0 copy-done
  23.0 0.1 collective-permute-start
  23.1 0.5 collective-permute-start.1
  23.6 0.1 collective-permute-start.2
  23.7 8.5 %collective-permute-done.d1_hbm = bf16[384,4096]{1,0:T(8,128)(2,1)S(1)} collective-permute-done((bf16[384,4096]{1,0:T(8,128)(2,1)S(1)}, bf16[384,4096]{1,0:T(8,128)(2,1)S(1)}, u32[]{:S(2)}, u32[]{:S(2)}) %collective-permute-start) | collective-permute-done | bytes 3145760 | tf_op jit(solution)/shard_map/ppermute | solution.py:327
  32.3 0.0 copy-start.1
  32.3 1.6 copy-done.1
  33.9 3.7 %collective-permute-done.1.g1_hbm = bf16[4096,384]{1,0:T(8,128)(2,1)S(1)} collective-permute-done((bf16[4096,384]{1,0:T(8,128)(2,1)}, bf16[4096,384]{1,0:T(8,128)(2,1)S(1)}, u32[]{:S(2)}, u32[]{:S(2)}) %collective-permute-start.1) | collective-permute-done | bytes 3145760 | tf_op jit(solution)/shard_map/ppermute | solution.py:327
  37.6 0.0 copy-start.2
  37.6 1.7 copy-done.2
  39.3 0.0 collective-permute-done.2.u1_hbm
  39.3 127.2 %all-to-all-done = bf16[128,192,128]{2,1,0:T(8,128)(2,1)} async-done(((bf16[128,192,128]{2,1,0:T(8,128)(2,1)}), bf16[128,192,128]{2,1,0:T(8,128)(2,1)}, u32[]{:S(2)}, u32[]{:S(2)}) %all-to-all-start) | async-done | bytes 6291488 | tf_op jit(solution)/shard_map/all_to_all | solution.py:318
  166.4 19.4 %expert_terms.1 = bf16[128,13,8,128]{3,2,1,0:T(8,128)(2,1)} custom-call(bf16[128,2,3,32,128]{4,3,2,1,0:T(8,128)(2,1)} %bitcast.3.x_hbm, bf16[384,4096]{1,0:T(8,128)(2,1)S(1)} %bitcast.12, bf16[384,4096]{1,0:T(8,128)(2,1)} %copy-done.1, bf16[4096,384]{1,0:T(8,128)(2,1)} %bitcast.16, bf16[4096,384]{1,0:T(8,128)(2,1)} %copy-done.2, bf16[4096,384]{1,0:T(8,128)(2,1)} %bitcast.18, ...), custom_call_target="tpu_custom_call" | custom-call | tf_op jit(solution)/shard_map/expert_terms/pallas_call | solution.py:242
  185.9 86.1 %all_to_all.10 = bf16[128,104,128]{2,1,0:T(8,128)(2,1)S(1)} all-to-all(bf16[128,104,128]{2,1,0:T(8,128)(2,1)} %bitcast.13), channel_id=1, replica_groups=mesh['seq'=2,'expert'=128] {'expert'}, dimensions={0} | all-to-all | bytes 6815744 | tf_op jit(solution)/shard_map/all_to_all | solution.py:318
  271.9 3.2 %combine.1 = (bf16[128,4096]{1,0:T(8,128)(2,1)}, bf16[2,128]{1,0:T(2,128)(2,1)}) custom-call(s32[2,128]{1,0:T(2,128)} %bitcast.20, s32[2,128]{1,0:T(2,128)} %get-tuple-element.6.position_ref, f32[2,128]{1,0:T(2,128)} %bitcast.21, bf16[128,13,8,128]{3,2,1,0:T(8,128)(2,1)S(1)} %bitcast.10), custom_call_target="tpu_custom_call" | custom-call | tf_op jit(solution)/shard_map/combine/pallas_call | solution.py:302
Async XLA Ops:
  7.3 15.7 %copy-start = (bf16[1,384,4096]{2,1,0:T(8,128)(2,1)S(1)}, bf16[1,384,4096]{2,1,0:T(8,128)(2,1)}, u32[]{:S(2)}) copy-start(bf16[1,384,4096]{2,1,0:T(8,128)(2,1)} %param.12) | copy-start | bytes 9437188
  7.3 159.1 %all-to-all-start = ((bf16[128,192,128]{2,1,0:T(8,128)(2,1)}), bf16[128,192,128]{2,1,0:T(8,128)(2,1)}, u32[]{:S(2)}, u32[]{:S(2)}) async-start(bf16[128,192,128]{2,1,0:T(8,128)(2,1)} %bitcast.14), calls=%async_computation | async-start | bytes 12582912 | tf_op jit(solution)/shard_map/all_to_all | solution.py:318
  23.0 9.2 %collective-permute-start = (bf16[384,4096]{1,0:T(8,128)(2,1)S(1)}, bf16[384,4096]{1,0:T(8,128)(2,1)S(1)}, u32[]{:S(2)}, u32[]{:S(2)}) collective-permute-start(bf16[384,4096]{1,0:T(8,128)(2,1)S(1)} %bitcast.11), channel_id=1, source_target_pairs={{0,128},{128,0},{1,129},{129,1},{2,130},{130,2},{3,131},{131,3},{4... | collective-permute-start | bytes 9437192 | tf_op jit(solution)/shard_map/ppermute | solution.py:327
  23.1 14.5 %collective-permute-start.1 = (bf16[4096,384]{1,0:T(8,128)(2,1)}, bf16[4096,384]{1,0:T(8,128)(2,1)S(1)}, u32[]{:S(2)}, u32[]{:S(2)}) collective-permute-start(bf16[4096,384]{1,0:T(8,128)(2,1)} %bitcast.15), channel_id=1, source_target_pairs={{0,128},{128,0},{1,129},{129,1},{2,130},{130,2},{3,131},{131,3},{4... | collective-permute-start | bytes 9437192 | tf_op jit(solution)/shard_map/ppermute | solution.py:327
  23.6 15.7 %collective-permute-start.2 = (bf16[4096,384]{1,0:T(8,128)(2,1)}, bf16[4096,384]{1,0:T(8,128)(2,1)}, u32[]{:S(2)}, u32[]{:S(2)}) collective-permute-start(bf16[4096,384]{1,0:T(8,128)(2,1)} %bitcast.17), channel_id=1, source_target_pairs={{0,128},{128,0},{1,129},{129,1},{2,130},{130,2},{3,131},{131,3},{4... | collective-permute-start | bytes 9437192 | tf_op jit(solution)/shard_map/ppermute | solution.py:327
  32.3 1.6 copy-start.1
  37.6 1.7 copy-start.2

commit v5 on v4

--- a/solution.py
+++ b/solution.py
@@ -12,6 +12,7 @@
 GROUP = 16
 AHEAD = 8
 BLOCKS = 1
+PIECES = 4
 MIB = 1024 * 1024
 VMEM = pl.BlockSpec(memory_space=pltpu.VMEM)
 SMEM = pl.BlockSpec(memory_space=pltpu.SMEM)
@@ -26,26 +27,36 @@
     return pltpu.with_memory_space_constraint(x, pltpu.VMEM)
 
 
-def place_rows(rows_ref, stage, slots_of):
+def place_rows(rows_ref, source, blocks, stage, send):
     tok_count = rows_ref.shape[0]
-    parts = stage.shape[2]
+    experts, capacity, parts, _ = stage.shape
+    for r in range(0, tok_count, GROUP):
+        blocks[r : r + GROUP] = rows_ref[r : r + GROUP, :].reshape(GROUP, parts, LANES)
+    group = 4
+    share = experts // PIECES
 
     def place(g, _):
-        first = pl.multiple_of(g * GROUP, GROUP)
-        rows = rows_ref[pl.ds(first, GROUP), :].reshape(GROUP, parts, LANES)
-        for i in range(GROUP):
-            for e, position in slots_of(first + i):
-                stage[e, position] = rows[i]
+        first = g * group
+        rows = [
+            [blocks[source[(first + i) * capacity + s]] for s in range(capacity)]
+            for i in range(group)
+        ]
+        for i in range(group):
+            for s in range(capacity):
+                stage[first + i, s] = rows[i][s]
         return 0
 
-    lax.fori_loop(0, tok_count // GROUP, place, 0)
+    for piece in range(PIECES):
+        lax.fori_loop(piece * share // group, (piece + 1) * share // group, place, 0)
+        send(piece, pl.ds(piece * share, share))
 
 
 def pack_kernel(
     routes_ref, tokens_hbm, grads_hbm, position_ref, out_ref,
-    counts, tokens_ref, grads_ref, stage_in, stage_grad, sems,
+    counts, source, tokens_ref, grads_ref, blocks, stage_in, stage_grad, sems,
 ):
-    top = routes_ref.shape[0]
+    top, tok_count = routes_ref.shape
+    capacity = stage_in.shape[1]
     load_in = pltpu.make_async_copy(tokens_hbm, tokens_ref, sems.at[0])
     load_grad = pltpu.make_async_copy(grads_hbm, grads_ref, sems.at[1])
     load_in.start()
@@ -53,33 +64,40 @@
 
     def clear(e, _):
         counts[e] = 0
+        for s in range(capacity):
+            source[e * capacity + s] = 0
         return 0
 
-    lax.fori_loop(0, counts.shape[0], clear, 0, unroll=16)
-
-    def ranked(t):
-        slots = []
+    lax.fori_loop(0, counts.shape[0], clear, 0, unroll=8)
+
+    def rank(t, _):
         for k in range(top):
             e = routes_ref[k, t]
             position = counts[e]
             counts[e] = position + 1
             position_ref[k, t] = position
-            slots.append((e, position))
-        return slots
-
-    def known(t):
-        return [(routes_ref[k, t], position_ref[k, t]) for k in range(top)]
+            source[e * capacity + position] = t
+        return 0
+
+    lax.fori_loop(0, tok_count, rank, 0, unroll=8)
+    sends = []
+
+    def sender(stage, which):
+        def send(piece, some):
+            copy = pltpu.make_async_copy(
+                stage.at[some], out_ref.at[some, which], sems.at[2 + which * PIECES + piece]
+            )
+            copy.start()
+            sends.append(copy)
+
+        return send
 
     load_in.wait()
-    place_rows(tokens_ref, stage_in, ranked)
-    send_in = pltpu.make_async_copy(stage_in, out_ref.at[:, 0], sems.at[2])
-    send_in.start()
+    place_rows(tokens_ref, source, blocks, stage_in, sender(stage_in, 0))
     load_grad.wait()
-    place_rows(grads_ref, stage_grad, known)
-    send_grad = pltpu.make_async_copy(stage_grad, out_ref.at[:, 1], sems.at[3])
-    send_grad.start()
-    send_in.wait()
-    send_grad.wait()
+    place_rows(grads_ref, source, blocks, stage_grad, sender(stage_grad, 1))
+    for copy in sends:
+        copy.wait()
 
 
 def pack(routes, tokens, grads, expert_count, capacity):
@@ -96,11 +114,13 @@
         out_specs=(SMEM, ANYWHERE),
         scratch_shapes=[
             pltpu.SMEM((expert_count,), jnp.int32),
+            pltpu.SMEM((expert_count * capacity,), jnp.int32),
             pltpu.VMEM((tok_count, width), jnp.bfloat16),
             pltpu.VMEM((tok_count, width), jnp.bfloat16),
+            pltpu.VMEM((tok_count, parts, LANES), jnp.bfloat16),
             stage,
             stage,
-            pltpu.SemaphoreType.DMA((4,)),
+            pltpu.SemaphoreType.DMA((2 + 2 * PIECES,)),
         ],
         compiler_params=params(62),
         name="pack",

time: 275 us -> 275 us (level)
  no operation moved by 1% of the time
where the time goes in v5:
time: 275 us; the launch traced here: 274 us
  waiting for transfers between devices  139 us (51%)
  blocking collectives  86.1 us (31%)
  Pallas kernels  28.6 us (10%)
  starting transfers between devices  16.4 us (6%)
  local copies, waits for them, and re-layouts  3.3 us (1%)
    all_to_all x1, waiting for transfers between devices, exchange(): lax.all_to_all(sent, 'expert', split_axis=0, concat_axis=0, tiled=True)  127 us
    all_to_all x1, blocking collectives, exchange(): lax.all_to_all(sent, 'expert', split_axis=0, concat_axis=0, tiled=True)  86.1 us
    pallas_call x1, Pallas kernels, expert_terms(): pl.pallas_call(expert_kernel, out_shape=jax.ShapeDtypeStruct((expert_coun...  19.4 us
    all_to_all x1, starting transfers between devices, exchange(): lax.all_to_all(sent, 'expert', split_axis=0, concat_axis=0, tiled=True)  15.7 us
    ppermute x3, waiting for transfers between devices, on_device(): swap = lambda w: lax.ppermute(w, 'seq', [(0, 1), (1, 0)])  12.3 us
    pallas_call x1, Pallas kernels, pack(): pl.pallas_call(pack_kernel, out_shape=(jax.ShapeDtypeStruct(routes.shape,...  6.07 us
  transfers between devices with their start and end apart: 4, of which 3 were waited for; matrix products, arithmetic and copies ran while one was open for 0% of the time, Pallas kernels for 0%

profile of v5, /device:TPU:32, one launch (start us, length us, event | category | flops | bytes accessed | tf_op | source)
XLA Modules:
  0.0 274.5 jit_solution(11813228314650435210)
XLA Ops:
  0.6 6.1 %pack.1 = (s32[2,128]{1,0:T(2,128)}, bf16[128,2,3,32,128]{4,3,2,1,0:T(8,128)(2,1)}) custom-call(s32[2,128]{1,0:T(2,128)} %bitcast.19, bf16[128,4096]{1,0:T(8,128)(2,1)} %tokens_hbm.1, bf16[128,4096]{1,0:T(8,128)(2,1)} %grads_hbm.1), custom_call_target="tpu_custom_call" | custom-call | tf_op jit(solution)/shard_map/pack/pallas_call | solution.py:107
  6.7 0.0 copy-start
  6.7 15.7 %all-to-all-start = ((bf16[128,192,128]{2,1,0:T(8,128)(2,1)}), bf16[128,192,128]{2,1,0:T(8,128)(2,1)}, u32[]{:S(2)}, u32[]{:S(2)}) async-start(bf16[128,192,128]{2,1,0:T(8,128)(2,1)} %bitcast.14), calls=%async_computation | async-start | bytes 12582912 | tf_op jit(solution)/shard_map/all_to_all | solution.py:338
  22.4 0.0 copy-done
  22.4 0.1 collective-permute-start
  22.5 0.5 collective-permute-start.1
  23.0 0.1 collective-permute-start.2
  23.1 8.5 %collective-permute-done.d1_hbm = bf16[384,4096]{1,0:T(8,128)(2,1)S(1)} collective-permute-done((bf16[384,4096]{1,0:T(8,128)(2,1)S(1)}, bf16[384,4096]{1,0:T(8,128)(2,1)S(1)}, u32[]{:S(2)}, u32[]{:S(2)}) %collective-permute-start) | collective-permute-done | bytes 3145760 | tf_op jit(solution)/shard_map/ppermute | solution.py:347
  31.7 0.0 copy-start.1
  31.7 1.6 copy-done.1
  33.3 3.7 %collective-permute-done.1.g1_hbm = bf16[4096,384]{1,0:T(8,128)(2,1)S(1)} collective-permute-done((bf16[4096,384]{1,0:T(8,128)(2,1)}, bf16[4096,384]{1,0:T(8,128)(2,1)S(1)}, u32[]{:S(2)}, u32[]{:S(2)}) %collective-permute-start.1) | collective-permute-done | bytes 3145760 | tf_op jit(solution)/shard_map/ppermute | solution.py:347
  37.0 0.0 copy-start.2
  37.0 1.7 copy-done.2
  38.7 0.0 collective-permute-done.2.u1_hbm
  38.7 127.2 %all-to-all-done = bf16[128,192,128]{2,1,0:T(8,128)(2,1)} async-done(((bf16[128,192,128]{2,1,0:T(8,128)(2,1)}), bf16[128,192,128]{2,1,0:T(8,128)(2,1)}, u32[]{:S(2)}, u32[]{:S(2)}) %all-to-all-start) | async-done | bytes 6291488 | tf_op jit(solution)/shard_map/all_to_all | solution.py:338
  165.8 19.4 %expert_terms.1 = bf16[128,13,8,128]{3,2,1,0:T(8,128)(2,1)} custom-call(bf16[128,2,3,32,128]{4,3,2,1,0:T(8,128)(2,1)} %bitcast.3.x_hbm, bf16[384,4096]{1,0:T(8,128)(2,1)S(1)} %bitcast.12, bf16[384,4096]{1,0:T(8,128)(2,1)} %copy-done.1, bf16[4096,384]{1,0:T(8,128)(2,1)} %bitcast.16, bf16[4096,384]{1,0:T(8,128)(2,1)} %copy-done.2, bf16[4096,384]{1,0:T(8,128)(2,1)} %bitcast.18, ...), custom_call_target="tpu_custom_call" | custom-call | tf_op jit(solution)/shard_map/expert_terms/pallas_call | solution.py:262
  185.2 86.1 %all_to_all.10 = bf16[128,104,128]{2,1,0:T(8,128)(2,1)S(1)} all-to-all(bf16[128,104,128]{2,1,0:T(8,128)(2,1)} %bitcast.13), channel_id=1, replica_groups=mesh['seq'=2,'expert'=128] {'expert'}, dimensions={0} | all-to-all | bytes 6815744 | tf_op jit(solution)/shard_map/all_to_all | solution.py:338
  271.3 3.2 %combine.1 = (bf16[128,4096]{1,0:T(8,128)(2,1)}, bf16[2,128]{1,0:T(2,128)(2,1)}) custom-call(s32[2,128]{1,0:T(2,128)} %bitcast.20, s32[2,128]{1,0:T(2,128)} %get-tuple-element.6.position_ref, f32[2,128]{1,0:T(2,128)} %bitcast.21, bf16[128,13,8,128]{3,2,1,0:T(8,128)(2,1)S(1)} %bitcast.10), custom_call_target="tpu_custom_call" | custom-call | tf_op jit(solution)/shard_map/combine/pallas_call | solution.py:322
Async XLA Ops:
  6.7 15.7 %copy-start = (bf16[1,384,4096]{2,1,0:T(8,128)(2,1)S(1)}, bf16[1,384,4096]{2,1,0:T(8,128)(2,1)}, u32[]{:S(2)}) copy-start(bf16[1,384,4096]{2,1,0:T(8,128)(2,1)} %param.12) | copy-start | bytes 9437188
  6.7 159.1 %all-to-all-start = ((bf16[128,192,128]{2,1,0:T(8,128)(2,1)}), bf16[128,192,128]{2,1,0:T(8,128)(2,1)}, u32[]{:S(2)}, u32[]{:S(2)}) async-start(bf16[128,192,128]{2,1,0:T(8,128)(2,1)} %bitcast.14), calls=%async_computation | async-start | bytes 12582912 | tf_op jit(solution)/shard_map/all_to_all | solution.py:338
  22.4 9.2 %collective-permute-start = (bf16[384,4096]{1,0:T(8,128)(2,1)S(1)}, bf16[384,4096]{1,0:T(8,128)(2,1)S(1)}, u32[]{:S(2)}, u32[]{:S(2)}) collective-permute-start(bf16[384,4096]{1,0:T(8,128)(2,1)S(1)} %bitcast.11), channel_id=1, source_target_pairs={{0,128},{128,0},{1,129},{129,1},{2,130},{130,2},{3,131},{131,3},{4... | collective-permute-start | bytes 9437192 | tf_op jit(solution)/shard_map/ppermute | solution.py:347
  22.5 14.5 %collective-permute-start.1 = (bf16[4096,384]{1,0:T(8,128)(2,1)}, bf16[4096,384]{1,0:T(8,128)(2,1)S(1)}, u32[]{:S(2)}, u32[]{:S(2)}) collective-permute-start(bf16[4096,384]{1,0:T(8,128)(2,1)} %bitcast.15), channel_id=1, source_target_pairs={{0,128},{128,0},{1,129},{129,1},{2,130},{130,2},{3,131},{131,3},{4... | collective-permute-start | bytes 9437192 | tf_op jit(solution)/shard_map/ppermute | solution.py:347
  23.0 15.7 %collective-permute-start.2 = (bf16[4096,384]{1,0:T(8,128)(2,1)}, bf16[4096,384]{1,0:T(8,128)(2,1)}, u32[]{:S(2)}, u32[]{:S(2)}) collective-permute-start(bf16[4096,384]{1,0:T(8,128)(2,1)} %bitcast.17), channel_id=1, source_target_pairs={{0,128},{128,0},{1,129},{129,1},{2,130},{130,2},{3,131},{131,3},{4... | collective-permute-start | bytes 9437192 | tf_op jit(solution)/shard_map/ppermute | solution.py:347
  31.7 1.6 copy-start.1
  37.0 1.7 copy-start.2

commit v6 on v5

--- a/solution.py
+++ b/solution.py
@@ -144,6 +144,11 @@
     def cut(step):
         return pl.ds(step * depth, depth)
 
+    def halves(step):
+        if step:
+            return [cut(step)]
+        return [pl.ds(0, depth // 2), pl.ds(depth // 2, depth // 2)]
+
     count = [0]
 
     def fetch(src, dst):
@@ -156,7 +161,8 @@
     batches = [
         [fetch_rows(0, step)]
         + [
-            fetch(src.at[cut(step)], gate_up.at[cut(step), pl.ds(h * half, half)])
+            fetch(src.at[rows_in], gate_up.at[rows_in, pl.ds(h * half, half)])
+            for rows_in in halves(step)
             for h, src in enumerate((g0_hbm, g1_hbm, u0_hbm, u1_hbm))
         ]
         for step in range(steps)
@@ -185,11 +191,25 @@
 
     both = None
     for step in range(steps):
+        if step == 0:
+            for copy in batches[0][:5]:
+                copy.wait()
+            got = taken(0, 0, 0, experts)
+            both = jnp.dot(
+                got[:, : depth // 2], gate_up[: depth // 2], preferred_element_type=jnp.float32
+            )
+            for copy in batches[0][5:]:
+                copy.wait()
+            both = both + jnp.dot(
+                got[:, depth // 2 :],
+                gate_up[depth // 2 : depth],
+                preferred_element_type=jnp.float32,
+            )
+            continue
         arrive(step)
-        part = jnp.dot(
+        both = both + jnp.dot(
             taken(0, step, 0, experts), gate_up[cut(step)], preferred_element_type=jnp.float32
         )
-        both = part if step == 0 else both + part
     wide[...] = both
     for step in range(steps):
         arrive(steps + step)
@@ -272,7 +292,7 @@
             pltpu.VMEM((rows, 2 * hid), jnp.float32),
             pltpu.VMEM((max(rows, expert_count * CHUNK), LANES), jnp.float32),
             pltpu.VMEM((expert_count, tiles, CHUNK, LANES), jnp.bfloat16),
-            pltpu.SemaphoreType.DMA((8 * steps,)),
+            pltpu.SemaphoreType.DMA((8 * steps + 4,)),
             pltpu.SemaphoreType.DMA((BLOCKS * (tiles - 1) + 1,)),
         ],
         compiler_params=params(50),

time: 275 us -> 274 us (level)
  no operation moved by 1% of the time
where the time goes in v6:
time: 274 us
  waiting for transfers between devices  139 us (51%)
  blocking collectives  86 us (31%)
  Pallas kernels  27.7 us (10%)
  starting transfers between devices  16.4 us (6%)
  local copies, waits for them, and re-layouts  3.3 us (1%)
    all_to_all x1, waiting for transfers between devices, exchange(): lax.all_to_all(sent, 'expert', split_axis=0, concat_axis=0, tiled=True)  127 us
    all_to_all x1, blocking collectives, exchange(): lax.all_to_all(sent, 'expert', split_axis=0, concat_axis=0, tiled=True)  86 us
    pallas_call x1, Pallas kernels, expert_terms(): pl.pallas_call(expert_kernel, out_shape=jax.ShapeDtypeStruct((expert_coun...  18.5 us
    all_to_all x1, starting transfers between devices, exchange(): lax.all_to_all(sent, 'expert', split_axis=0, concat_axis=0, tiled=True)  15.7 us
    ppermute x3, waiting for transfers between devices, on_device(): swap = lambda w: lax.ppermute(w, 'seq', [(0, 1), (1, 0)])  12.3 us
    pallas_call x1, Pallas kernels, pack(): pl.pallas_call(pack_kernel, out_shape=(jax.ShapeDtypeStruct(routes.shape,...  6.07 us
  transfers between devices with their start and end apart: 4, of which 3 were waited for; matrix products, arithmetic and copies ran while one was open for 0% of the time, Pallas kernels for 0%

profile of v6, /device:TPU:32, one launch (start us, length us, event | category | flops | bytes accessed | tf_op | source)
XLA Modules:
  0.0 273.6 jit_solution(1324715809838523287)
XLA Ops:
  0.6 6.1 %pack.1 = (s32[2,128]{1,0:T(2,128)}, bf16[128,2,3,32,128]{4,3,2,1,0:T(8,128)(2,1)}) custom-call(s32[2,128]{1,0:T(2,128)} %bitcast.19, bf16[128,4096]{1,0:T(8,128)(2,1)} %tokens_hbm.1, bf16[128,4096]{1,0:T(8,128)(2,1)} %grads_hbm.1), custom_call_target="tpu_custom_call" | custom-call | tf_op jit(solution)/shard_map/pack/pallas_call | solution.py:107
  6.7 0.0 copy-start
  6.7 15.7 %all-to-all-start = ((bf16[128,192,128]{2,1,0:T(8,128)(2,1)}), bf16[128,192,128]{2,1,0:T(8,128)(2,1)}, u32[]{:S(2)}, u32[]{:S(2)}) async-start(bf16[128,192,128]{2,1,0:T(8,128)(2,1)} %bitcast.14), calls=%async_computation | async-start | bytes 12582912 | tf_op jit(solution)/shard_map/all_to_all | solution.py:358
  22.4 0.0 copy-done
  22.4 0.1 collective-permute-start
  22.5 0.5 collective-permute-start.1
  23.0 0.1 collective-permute-start.2
  23.1 8.5 %collective-permute-done.d1_hbm = bf16[384,4096]{1,0:T(8,128)(2,1)S(1)} collective-permute-done((bf16[384,4096]{1,0:T(8,128)(2,1)S(1)}, bf16[384,4096]{1,0:T(8,128)(2,1)S(1)}, u32[]{:S(2)}, u32[]{:S(2)}) %collective-permute-start) | collective-permute-done | bytes 3145760 | tf_op jit(solution)/shard_map/ppermute | solution.py:367
  31.7 0.0 copy-start.1
  31.7 1.6 copy-done.1
  33.3 3.7 %collective-permute-done.1.g1_hbm = bf16[4096,384]{1,0:T(8,128)(2,1)S(1)} collective-permute-done((bf16[4096,384]{1,0:T(8,128)(2,1)}, bf16[4096,384]{1,0:T(8,128)(2,1)S(1)}, u32[]{:S(2)}, u32[]{:S(2)}) %collective-permute-start.1) | collective-permute-done | bytes 3145760 | tf_op jit(solution)/shard_map/ppermute | solution.py:367
  37.0 0.0 copy-start.2
  37.0 1.7 copy-done.2
  38.7 0.0 collective-permute-done.2.u1_hbm
  38.7 127.2 %all-to-all-done = bf16[128,192,128]{2,1,0:T(8,128)(2,1)} async-done(((bf16[128,192,128]{2,1,0:T(8,128)(2,1)}), bf16[128,192,128]{2,1,0:T(8,128)(2,1)}, u32[]{:S(2)}, u32[]{:S(2)}) %all-to-all-start) | async-done | bytes 6291488 | tf_op jit(solution)/shard_map/all_to_all | solution.py:358
  165.8 18.5 %expert_terms.1 = bf16[128,13,8,128]{3,2,1,0:T(8,128)(2,1)} custom-call(bf16[128,2,3,32,128]{4,3,2,1,0:T(8,128)(2,1)} %bitcast.3.x_hbm, bf16[384,4096]{1,0:T(8,128)(2,1)S(1)} %bitcast.12, bf16[384,4096]{1,0:T(8,128)(2,1)} %copy-done.1, bf16[4096,384]{1,0:T(8,128)(2,1)} %bitcast.16, bf16[4096,384]{1,0:T(8,128)(2,1)} %copy-done.2, bf16[4096,384]{1,0:T(8,128)(2,1)} %bitcast.18, ...), custom_call_target="tpu_custom_call" | custom-call | tf_op jit(solution)/shard_map/expert_terms/pallas_call | solution.py:282
  184.3 86.0 %all_to_all.10 = bf16[128,104,128]{2,1,0:T(8,128)(2,1)S(1)} all-to-all(bf16[128,104,128]{2,1,0:T(8,128)(2,1)} %bitcast.13), channel_id=1, replica_groups=mesh['seq'=2,'expert'=128] {'expert'}, dimensions={0} | all-to-all | bytes 6815744 | tf_op jit(solution)/shard_map/all_to_all | solution.py:358
  270.4 3.2 %combine.1 = (bf16[128,4096]{1,0:T(8,128)(2,1)}, bf16[2,128]{1,0:T(2,128)(2,1)}) custom-call(s32[2,128]{1,0:T(2,128)} %bitcast.20, s32[2,128]{1,0:T(2,128)} %get-tuple-element.6.position_ref, f32[2,128]{1,0:T(2,128)} %bitcast.21, bf16[128,13,8,128]{3,2,1,0:T(8,128)(2,1)S(1)} %bitcast.10), custom_call_target="tpu_custom_call" | custom-call | tf_op jit(solution)/shard_map/combine/pallas_call | solution.py:342
Async XLA Ops:
  6.7 15.7 %copy-start = (bf16[1,384,4096]{2,1,0:T(8,128)(2,1)S(1)}, bf16[1,384,4096]{2,1,0:T(8,128)(2,1)}, u32[]{:S(2)}) copy-start(bf16[1,384,4096]{2,1,0:T(8,128)(2,1)} %param.12) | copy-start | bytes 9437188
  6.7 159.1 %all-to-all-start = ((bf16[128,192,128]{2,1,0:T(8,128)(2,1)}), bf16[128,192,128]{2,1,0:T(8,128)(2,1)}, u32[]{:S(2)}, u32[]{:S(2)}) async-start(bf16[128,192,128]{2,1,0:T(8,128)(2,1)} %bitcast.14), calls=%async_computation | async-start | bytes 12582912 | tf_op jit(solution)/shard_map/all_to_all | solution.py:358
  22.4 9.2 %collective-permute-start = (bf16[384,4096]{1,0:T(8,128)(2,1)S(1)}, bf16[384,4096]{1,0:T(8,128)(2,1)S(1)}, u32[]{:S(2)}, u32[]{:S(2)}) collective-permute-start(bf16[384,4096]{1,0:T(8,128)(2,1)S(1)} %bitcast.11), channel_id=1, source_target_pairs={{0,128},{128,0},{1,129},{129,1},{2,130},{130,2},{3,131},{131,3},{4... | collective-permute-start | bytes 9437192 | tf_op jit(solution)/shard_map/ppermute | solution.py:367
  22.5 14.5 %collective-permute-start.1 = (bf16[4096,384]{1,0:T(8,128)(2,1)}, bf16[4096,384]{1,0:T(8,128)(2,1)S(1)}, u32[]{:S(2)}, u32[]{:S(2)}) collective-permute-start(bf16[4096,384]{1,0:T(8,128)(2,1)} %bitcast.15), channel_id=1, source_target_pairs={{0,128},{128,0},{1,129},{129,1},{2,130},{130,2},{3,131},{131,3},{4... | collective-permute-start | bytes 9437192 | tf_op jit(solution)/shard_map/ppermute | solution.py:367
  23.0 15.7 %collective-permute-start.2 = (bf16[4096,384]{1,0:T(8,128)(2,1)}, bf16[4096,384]{1,0:T(8,128)(2,1)}, u32[]{:S(2)}, u32[]{:S(2)}) collective-permute-start(bf16[4096,384]{1,0:T(8,128)(2,1)} %bitcast.17), channel_id=1, source_target_pairs={{0,128},{128,0},{1,129},{129,1},{2,130},{130,2},{3,131},{131,3},{4... | collective-permute-start | bytes 9437192 | tf_op jit(solution)/shard_map/ppermute | solution.py:367
  31.7 1.6 copy-start.1
  37.0 1.7 copy-start.2
